TPU v7x, 1024 devices: a whole 8x8x8 slice. The times are simulated.
1024 devices in a mesh: section: 128 (over y, z_hi, x), tensor: 8 (over z_lo, core).
Axes of the slice: x: 8, y: 8, z: 8 (z_hi: 2, z_lo: 4; z = z_hi * 4 + z_lo), core: 2. Of those that a mesh axis runs over, the one named last changes fastest.
Arguments:
- produced: bfloat16 [128, 2, 192, 8192], P('section', None, None, 'tensor'), may hold values from -7 to 7
- saved_inputs: bfloat16 [128, 192, 8192], P('section', None, 'tensor'), may hold values from -7 to 7
- upstream: bfloat16 [128, 192, 8192], P('section', None, 'tensor'), may hold values from -6 to 6
- norm_gain: float32 [128, 8192], P('section', 'tensor'), may hold values from 0.1 to 1.9
- w_key: bfloat16 [128, 8, 1024, 128], P('section', 'tensor'), may hold values from -22 to 22
- w_value: bfloat16 [128, 8, 1024, 128], P('section', 'tensor'), may hold values from -0.1875 to 0.1875
- batch_order: int32 [128], replicated, may hold values from 0 to 1
- segment_ids: int32 [2, 192], replicated, may hold values from 0 to 3, never falling along the last dimension, each value on 1 to 96 neighbouring positions
Outputs:
- forward_out: bfloat16 [128, 192, 8192], P('section', None, 'tensor')
- input_grad: bfloat16 [128, 192, 8192], P('section', None, 'tensor')
Inputs may be any that keep to these rules, and one draw needn't show every extreme that they name: `segment_ids`: each row numbers the documents of one micro-batch in order; a document's tokens are contiguous.
All inputs are finite; a program needn't handle non-finite values.
Results may differ from a plain program's by a relative error of at most 0.0055.
The roundings to bfloat16 on the way count: a program that leaves them out, or rounds other values in their place, can miss the bound.
Values may be sent and summed in bfloat16 or wider, within the bound.
A program may use at most 32 MiB of HBM per device.

v0:
```python
import jax
import jax.numpy as jnp
from jax import lax
from jax.sharding import PartitionSpec as P

D = 8192


EPSILON = 1e-05


def from_behind(block, axis, distance):
    devices = range(lax.axis_size(axis))
    route = [((i - distance) % len(devices), i) for i in devices]
    return lax.ppermute(block, axis, route)


def attention_parts(normed, key_weights, value_weights, segment):
    length = normed.shape[0]
    group_count = key_weights.shape[0]
    head_size = key_weights.shape[2]
    grouped = normed.reshape(length, group_count, -1)
    queries = normed.reshape(length, group_count, -1, head_size)
    key_rows = jnp.einsum(
        "lke,ked->lkd", grouped, key_weights, preferred_element_type=jnp.float32
    ).astype(jnp.bfloat16)
    value_rows = jnp.einsum(
        "lke,ked->lkd", grouped, value_weights, preferred_element_type=jnp.float32
    ).astype(jnp.bfloat16)
    score_scale = head_size ** (-0.5)
    scores = (
        jnp.einsum("lkgd,mkd->kglm", queries, key_rows, preferred_element_type=jnp.float32)
        * score_scale
    )
    position = jnp.arange(length)
    allowed = (position[None, :] <= position[:, None]) & (segment[:, None] == segment[None, :])
    scores = jnp.where(allowed[None, None], scores, -jnp.inf)
    attn_weights = jax.nn.softmax(scores, axis=-1)
    return (queries, key_rows, value_rows, attn_weights, score_scale)


def on_device(
    produced, saved_inputs, upstream, norm_gain, w_key, w_value, batch_order, segment_ids
):
    section_index = lax.axis_index("section")
    forward_batch = lax.dynamic_index_in_dim(batch_order, section_index, 0, keepdims=False)
    arrived = from_behind(produced[0], "section", 1)
    forward_in = lax.dynamic_index_in_dim(arrived, forward_batch, 0, keepdims=False)
    grad_rows = from_behind(upstream[0], "section", -1)
    backward_in = saved_inputs[0]
    gain_row = norm_gain[0]
    key_weights = w_key[0]
    value_weights = w_value[0]
    segment_forward = lax.dynamic_index_in_dim(segment_ids, forward_batch, 0, keepdims=False)
    segment_backward = lax.dynamic_index_in_dim(segment_ids, 1 - forward_batch, 0, keepdims=False)
    forward_wide = forward_in.astype(jnp.float32)
    backward_wide = backward_in.astype(jnp.float32)
    squares_forward, squares_backward = lax.psum(
        (
            jnp.sum(forward_wide * forward_wide, axis=-1),
            jnp.sum(backward_wide * backward_wide, axis=-1),
        ),
        "tensor",
    )
    forward_scale = lax.rsqrt(squares_forward / D + EPSILON)
    backward_scale = lax.rsqrt(squares_backward / D + EPSILON)
    forward_normed = (forward_wide * forward_scale[:, None] * gain_row[None, :]).astype(
        jnp.bfloat16
    )
    queries, key_rows, value_rows, attn_weights, score_scale = attention_parts(
        forward_normed, key_weights, value_weights, segment_forward
    )
    rounded = attn_weights.astype(jnp.bfloat16)
    mixed_heads = jnp.einsum(
        "kglm,mkd->lkgd", rounded, value_rows, preferred_element_type=jnp.float32
    ).astype(jnp.bfloat16)
    forward_rows = (
        forward_wide + mixed_heads.reshape(forward_in.shape).astype(jnp.float32)
    ).astype(jnp.bfloat16)
    backward_normed = (backward_wide * backward_scale[:, None] * gain_row[None, :]).astype(
        jnp.bfloat16
    )
    queries, key_rows, value_rows, attn_weights, score_scale = attention_parts(
        backward_normed, key_weights, value_weights, segment_backward
    )
    rounded = attn_weights.astype(jnp.bfloat16)
    length = backward_in.shape[0]
    group_count = key_weights.shape[0]
    out_grad = grad_rows.reshape(queries.shape)
    value_grad = jnp.einsum(
        "kglm,lkgd->mkd", rounded, out_grad, preferred_element_type=jnp.float32
    ).astype(jnp.bfloat16)
    weight_grad = jnp.einsum(
        "lkgd,mkd->kglm", out_grad, value_rows, preferred_element_type=jnp.float32
    )
    row_terms = jnp.sum(weight_grad * attn_weights, axis=-1, keepdims=True)
    score_grad = (attn_weights * (weight_grad - row_terms) * score_scale).astype(jnp.bfloat16)
    query_grad = jnp.einsum(
        "kglm,mkd->lkgd", score_grad, key_rows, preferred_element_type=jnp.float32
    )
    key_grad = jnp.einsum(
        "kglm,lkgd->mkd", score_grad, queries, preferred_element_type=jnp.float32
    ).astype(jnp.bfloat16)
    normed_grad = query_grad.reshape(length, group_count, -1)
    normed_grad = normed_grad + jnp.einsum(
        "lkd,ked->lke", key_grad, key_weights, preferred_element_type=jnp.float32
    )
    normed_grad = normed_grad + jnp.einsum(
        "lkd,ked->lke", value_grad, value_weights, preferred_element_type=jnp.float32
    )
    normed_grad = normed_grad.reshape(backward_in.shape)
    inner_sums = lax.psum(
        jnp.sum(normed_grad * gain_row[None, :] * backward_wide, axis=-1), "tensor"
    )
    stream_grad = (
        backward_scale[:, None] * gain_row[None, :] * normed_grad
        - backward_wide * (backward_scale**3 / D * inner_sums)[:, None]
    )
    backward_rows = (grad_rows.astype(jnp.float32) + stream_grad).astype(jnp.bfloat16)
    return (forward_rows[None], backward_rows[None])


def solution(mesh):
    return jax.shard_map(
        on_device,
        mesh=mesh,
        in_specs=(
            P("section", None, None, "tensor"),
            P("section", None, "tensor"),
            P("section", None, "tensor"),
            P("section", "tensor"),
            P("section", "tensor", None, None),
            P("section", "tensor", None, None),
            P(),
            P(),
        ),
        out_specs=(P("section", None, "tensor"), P("section", None, "tensor")),
        check_vma=False,
    )
```

profile of v0, /device:TPU:1, one launch (start us, length us, event | category | flops | bytes accessed | tf_op | source)
XLA Modules:
  0.0 106.8 jit_solution(17388271004610097245)
XLA Ops:
  0.6 0.0 copy-start
  0.6 0.0 copy-start.1
  0.7 0.0 copy-start.7
  0.7 0.0 copy-start.6
  0.7 0.0 copy-start.5
  0.7 0.0 copy-start.4
  0.7 21.2 %collective-permute-start.1 = (bf16[192,1024]{1,0:T(8,128)(2,1)}, bf16[192,1024]{1,0:T(8,128)(2,1)S(1)}, u32[]{:S(2)}, u32[]{:S(2)}) collective-permute-start(bf16[192,1024]{1,0:T(8,128)(2,1)} %bitcast.258), channel_id=1, source_target_pairs={{8,0},{16,8},{24,16},{32,24},{40,32},{48,40},{56,48},{64,56},{72,6... | collective-permute-start | bytes 1179656 | tf_op jit(solution)/shard_map/ppermute | solution.py:15
  21.9 1.9 %collective-permute-start = (bf16[2,192,1024]{2,1,0:T(8,128)(2,1)}, bf16[2,192,1024]{2,1,0:T(8,128)(2,1)}, u32[]{:S(2)}, u32[]{:S(2)}) collective-permute-start(bf16[2,192,1024]{2,1,0:T(8,128)(2,1)} %bitcast.257), channel_id=1, source_target_pairs={{1016,0},{0,8},{8,16},{16,24},{24,32},{32,40},{40,48},{48,56},{56,... | collective-permute-start | bytes 2359304 | tf_op jit(solution)/shard_map/ppermute | solution.py:15
  23.9 1.2 %fusion.23 = f32[192]{0:T(256)S(1)} fusion(bf16[1,192,1024]{2,1,0:T(8,128)(2,1)} %param.9), kind=kLoop, calls=%fused_computation.48 | loop fusion | flops 589632 | bytes 393984 | tf_op jit(solution)/shard_map/reduce_sum | solution.py:61
  25.0 1.1 %convert_bitcast_fusion = f32[24,8,8,128]{3,1,2,0:T(8,128)S(1)} fusion(bf16[1,192,1024]{2,1,0:T(8,128)(2,1)} %param.9), kind=kLoop, calls=%fused_computation.14 | loop fusion | flops 196608 | bytes 1179648
  26.1 0.0 copy-done.7
  26.1 0.6 dynamic_slice.15
  29.9 0.0 copy-done.6
  30.0 0.1 fusion.77
  30.1 35.0 %psum.22 = f32[192]{0:T(256)S(1)} all-reduce(f32[192]{0:T(256)S(1)} %fusion.23), channel_id=1, replica_groups=mesh['section'=128,'tensor'=8] {'tensor'}, use_global_device_ids=true, to_apply=%region_5.6 | all-reduce | flops 192 | bytes 1536 | tf_op jit(solution)/shard_map/psum | solution.py:58
  65.1 0.0 copy-done.1
  65.1 0.0 copy-done.5
  65.1 0.2 fusion.51
  65.3 0.0 copy-done.4
  65.3 0.3 fusion.20
  65.6 0.1 copy.29
  65.7 1.0 copy.30
  66.7 0.4 fusion.90
  67.1 0.3 fusion.6
  67.4 0.1 fusion.78
  67.5 0.0 collective-permute-done.1
  67.5 0.0 copy-done
  67.5 0.0 copy-start.2
  67.5 1.8 %fusion = (f32[8,192]{1,0:T(8,128)S(1)}, f32[192,192,8]{1,0,2:T(8,128)}) fusion(f32[8,192]{1,0:T(8,128)S(1)} %fusion.6, f32[1,8,192,192]{2,3,1,0:T(8,128)S(1)} %get-tuple-element.7, f32[8,192]{1,0:T(8,128)S(1)} %get-tuple-element.6, bf16[1,1,1024,128]{3,2,1,0:T(8,128)(2,1)S(1)} %copy-done, bf16[1,192,1024]{2,1,0:T(8,128)(2,1)S(1)} %copy-done.1, ...), kind=kOutput, calls=%fused_computation.4 | convolution fusion | flops 127818240 | bytes 3431168 | tf_op jit(solution)/shard_map/lkgd,mkd->kglm/dot_general | solution.py:93
  69.3 1.8 %fusion.40 = bf16[8,192,192]{1,2,0:T(8,128)(2,1)S(1)} fusion(f32[192,192,8]{1,0,2:T(8,128)} %get-tuple-element.9, f32[8,192]{1,0:T(8,128)S(1)} %get-tuple-element.8, f32[8,192]{1,0:T(8,128)S(1)} %fusion.6, f32[1,8,192,192]{2,3,1,0:T(8,128)S(1)} %get-tuple-element.7, f32[8,192]{1,0:T(8,128)S(1)} %get-tuple-element.6), kind=kLoop, calls=%fused_computation.65 | loop fusion | flops 1769472 | bytes 2967552 | tf_op jit(solution)/shard_map/reshape.44
  71.2 0.5 convolution_bitcast_fusion
  71.6 1.4 %copy.22 = f32[192,1,8,128]{3,2,1,0:T(8,128)} copy(f32[192,1,8,128]{3,0,2,1:T(8,128)S(1)} %convolution_bitcast_fusion) | data formatting | bytes 1572864 | tf_op jit(solution)/shard_map/kglm,mkd->lkgd/transpose | solution.py:98
  73.0 0.0 copy-done.2
  73.0 1.5 %convolution_bitcast_fusion.1 = f32[192,1,1024]{2,0,1:T(8,128)} fusion(bf16[1,1,1024,128]{3,2,1,0:T(8,128)(2,1)S(1)} %copy-done, f32[1,8,192,192]{2,3,1,0:T(8,128)S(1)} %get-tuple-element.7, f32[8,192]{1,0:T(8,128)S(1)} %fusion.6, f32[8,192]{1,0:T(8,128)S(1)} %get-tuple-element.6, bf16[192,1024]{1,0:T(8,128)(2,1)S(1)} %collective-permute-done.1), kind=kOutput, calls=%fused_computation.23 | convolution fusion | flops 126738432 | bytes 2633728 | tf_op jit(solution)/shard_map/lkd,ked->lke/dot_general | solution.py:108
  74.5 2.6 %fusion.24 = (f32[192]{0:T(256)S(1)}, f32[192,1024]{1,0:T(8,128)S(1)}) fusion(bf16[1,192,1024]{2,1,0:T(8,128)(2,1)S(1)} %copy-done.1, f32[1024]{0:T(1024)S(1)} %bitcast.249, f32[192,1,1024]{2,0,1:T(8,128)} %convolution_bitcast_fusion.1, bf16[1,1,1024,128]{3,2,1,0:T(8,128)(2,1)} %param.12, bf16[8,192,192]{1,2,0:T(8,128)(2,1)S(1)} %fusion.40, ...), kind=kOutput, calls=%fused_computation.49 | convolution fusion | flops 127622976 | bytes 4400640 | tf_op jit(solution)/shard_map/lkd,ked->lke/dot_general | solution.py:105
  77.1 0.0 collective-permute-done
  77.1 1.2 %fusion.28 = f32[192]{0:T(256)S(1)} fusion(bf16[2,192,1024]{2,1,0:T(8,128)(2,1)} %collective-permute-done, s32[]{:T(128)S(6)} %select_n.21), kind=kLoop, calls=%fused_computation.53 | loop fusion | flops 589632 | bytes 393988 | tf_op jit(solution)/shard_map/reduce_sum | solution.py:60
  78.2 18.1 %all-reduce = (f32[192]{0:T(256)S(1)}, f32[192]{0:T(256)S(1)}) all-reduce(f32[192]{0:T(256)S(1)} %fusion.28, f32[192]{0:T(256)S(1)} %get-tuple-element.10), channel_id=1, replica_groups=mesh['section'=128,'tensor'=8] {'tensor'}, use_global_device_ids=true, to_apply=%region_1.2 | all-reduce | flops 384 | bytes 3072 | tf_op jit(solution)/shard_map/psum | solution.py:58
  96.3 1.2 %fusion.54 = bf16[24,8,8,128]{3,1,2,0:T(8,128)(2,1)S(1)} fusion(f32[1024]{0:T(1024)S(1)} %bitcast.251, f32[192]{0:T(256)S(1)} %get-tuple-element.15, bf16[2,192,1024]{2,1,0:T(8,128)(2,1)} %collective-permute-done, s32[]{:T(128)S(6)} %select_n.21), kind=kLoop, calls=%fused_computation.76 | loop fusion | flops 786432 | bytes 791300
  97.5 0.1 copy.28
  97.6 1.7 %fusion.97 = (f32[8,192]{1,0:T(8,128)S(1)}, f32[1,8,192,192]{2,3,1,0:T(8,128)S(1)}) fusion(bf16[192,8,128]{2,1,0:T(8,128)(2,1)S(1)} %bitcast.245, bf16[1,1,1024,128]{3,2,1,0:T(8,128)(2,1)} %param.12, f32[1024]{0:T(1024)S(1)} %bitcast.252, f32[192]{0:T(256)S(1)} %get-tuple-element.15, bf16[2,192,1024]{2,1,0:T(8,128)(2,1)} %collective-permute-done, ...), kind=kOutput, calls=%fused_computation.103 | convolution fusion | flops 127523328 | bytes 2276100 | tf_op jit(solution)/shard_map/lkgd,mkd->kglm/dot_general | solution.py:32
  99.3 0.3 fusion.4
  99.6 2.6 %fusion.12 = f32[192,1,8,128]{3,0,2,1:T(8,128)} fusion(f32[1,8,192,192]{2,3,1,0:T(8,128)S(1)} %get-tuple-element.13, f32[8,192]{1,0:T(8,128)S(1)} %fusion.4, f32[8,192]{1,0:T(8,128)S(1)} %get-tuple-element.12, bf16[1,1,1024,128]{3,2,1,0:T(8,128)(2,1)S(1)} %copy-done, f32[1024]{0:T(1024)S(1)} %bitcast.253, f32[192]{0:T(256)S(1)} %get-tuple-element.15, ...), kind=kOutput, calls=%fused_computation.31 | convolution fusion | flops 127918080 | bytes 2638596 | tf_op jit(solution)/shard_map/kglm,mkd->lkgd/dot_general | solution.py:74
  102.2 0.0 copy-start.3
  102.2 1.6 %copy.17 = f32[192,1,8,128]{3,2,1,0:T(8,128)S(1)} copy(f32[192,1,8,128]{3,0,2,1:T(8,128)} %fusion.12) | data formatting | bytes 1572864 | tf_op jit(solution)/shard_map/convert_element_type | solution.py:78
  103.8 2.0 %fusion.31 = bf16[1,192,1024]{2,1,0:T(8,128)(2,1)} fusion(f32[1,192,1024]{2,0,1:T(1,128)S(1)} %bitcast.241, bf16[2,192,1024]{2,1,0:T(8,128)(2,1)} %collective-permute-done, s32[]{:T(128)S(6)} %select_n.21), kind=kLoop, calls=%fused_computation.56 | loop fusion | flops 589824 | bytes 1572868 | tf_op jit(solution)/shard_map/convert_element_type | solution.py:79
  105.8 0.0 copy-done.3
  105.8 1.0 fusion.55
  (3 shorter events, 0.0 us)
Async XLA Ops:
  0.6 66.9 %copy-start = (bf16[1,1,1024,128]{3,2,1,0:T(8,128)(2,1)S(1)}, bf16[1,1,1024,128]{3,2,1,0:T(8,128)(2,1)}, u32[]{:S(2)}) copy-start(bf16[1,1,1024,128]{3,2,1,0:T(8,128)(2,1)} %param.13) | copy-start | bytes 786436
  0.6 64.4 %copy-start.1 = (bf16[1,192,1024]{2,1,0:T(8,128)(2,1)S(1)}, bf16[1,192,1024]{2,1,0:T(8,128)(2,1)}, u32[]{:S(2)}) copy-start(bf16[1,192,1024]{2,1,0:T(8,128)(2,1)} %param.9) | copy-start | bytes 1179652
  0.7 25.5 %copy-start.7 = (s32[128]{0:T(128)S(1)}, s32[128]{0:T(128)}, u32[]{:S(2)}) copy-start(s32[128]{0:T(128)} %param.14) | copy-start | bytes 1540
  0.7 29.3 %copy-start.6 = (s32[2,192]{1,0:T(2,128)S(1)}, s32[2,192]{1,0:T(2,128)}, u32[]{:S(2)}) copy-start(s32[2,192]{1,0:T(2,128)} %param.15) | copy-start | bytes 4612
  0.7 64.4 %copy-start.5 = (f32[1,1024]{1,0:T(1,128)S(1)}, f32[1,1024]{1,0:T(1,128)}, u32[]{:S(2)}) copy-start(f32[1,1024]{1,0:T(1,128)} %param.11) | copy-start | bytes 12292
  0.7 64.6 %copy-start.4 = (bf16[1,1,1024,128]{3,2,1,0:T(8,128)(2,1)S(1)}, bf16[1,1,1024,128]{3,2,1,0:T(8,128)(2,1)}, u32[]{:S(2)}) copy-start(bf16[1,1,1024,128]{3,2,1,0:T(8,128)(2,1)} %param.12) | copy-start | bytes 786436
  0.7 66.8 %collective-permute-start.1 = (bf16[192,1024]{1,0:T(8,128)(2,1)}, bf16[192,1024]{1,0:T(8,128)(2,1)S(1)}, u32[]{:S(2)}, u32[]{:S(2)}) collective-permute-start(bf16[192,1024]{1,0:T(8,128)(2,1)} %bitcast.258), channel_id=1, source_target_pairs={{8,0},{16,8},{24,16},{32,24},{40,32},{48,40},{56,48},{64,56},{72,6... | collective-permute-start | bytes 1179656 | tf_op jit(solution)/shard_map/ppermute | solution.py:15
  21.9 55.1 %collective-permute-start = (bf16[2,192,1024]{2,1,0:T(8,128)(2,1)}, bf16[2,192,1024]{2,1,0:T(8,128)(2,1)}, u32[]{:S(2)}, u32[]{:S(2)}) collective-permute-start(bf16[2,192,1024]{2,1,0:T(8,128)(2,1)} %bitcast.257), channel_id=1, source_target_pairs={{1016,0},{0,8},{8,16},{16,24},{24,32},{32,40},{40,48},{48,56},{56,... | collective-permute-start | bytes 2359304 | tf_op jit(solution)/shard_map/ppermute | solution.py:15
  67.5 5.5 %copy-start.2 = (bf16[192,1024]{1,0:T(8,128)(2,1)}, bf16[192,1024]{1,0:T(8,128)(2,1)S(1)}, u32[]{:S(2)}) copy-start(bf16[192,1024]{1,0:T(8,128)(2,1)S(1)} %collective-permute-done.1) | copy-start | bytes 1179652
  102.2 3.6 %copy-start.3 = (bf16[192,1024]{1,0:T(8,128)(2,1)S(1)}, bf16[192,1024]{1,0:T(8,128)(2,1)}, u32[]{:S(2)}) copy-start(bf16[192,1024]{1,0:T(8,128)(2,1)} %copy-done.2) | copy-start | bytes 1179652
where the time goes:
time: 107 us
  blocking collectives  53.1 us (50%)
  starting transfers between devices  23.2 us (22%)
  matrix products  11.4 us (11%)
  other arithmetic  10.2 us (10%)
  local copies, waits for them, and re-layouts  4.82 us (5%)
  between operations  4.12 us (4%)
    psum x2, blocking collectives, on_device(): lax.psum((jnp.sum(forward_wide * forward_wide, axis=-1), jnp.sum(backward...  53.1 us
    ppermute x2, starting transfers between devices, from_behind(): return lax.ppermute(block, axis, route)  23.2 us
    dot_general x1, matrix products, on_device(): jnp.einsum('kglm,mkd->lkgd', rounded, value_rows, preferred_element_type=...  2.59 us
    dot_general x1, matrix products, on_device(): jnp.einsum('lkd,ked->lke', key_grad, key_weights, preferred_element_type=...  2.56 us
    unnamed x3, other arithmetic  2.41 us
    dot_general x2, matrix products, attention_parts(): jnp.einsum('lkgd,mkd->kglm', queries, key_rows, preferred_element_type=jn...  2.15 us
  transfers between devices with their start and end apart: 2, of which 0 were waited for; matrix products, arithmetic and copies ran while one was open for 14% of the time, Pallas kernels for 0%

commit v1 on v0

v1 whole, which is shorter than its diff:
```python
import jax
import jax.numpy as jnp
from jax import lax
from jax.experimental import pallas as pl
from jax.experimental.pallas import tpu as pltpu
from jax.sharding import PartitionSpec as P

D = 8192
EPSILON = 1e-05
SECTIONS, TENSOR = 128, 8
SEQ, WIDTH, HEADS, HEAD = 192, 1024, 8, 128
SCALE = HEAD**-0.5
MESH = pl.DeviceIdType.MESH
F32, BF16 = jnp.float32, jnp.bfloat16
CHUNKS = ((0, 128), (128, 64))

UNITS = tuple((0, 128, (h,), 0) for h in range(HEADS)) + tuple(
    (q, 32, tuple(range(h, h + 4)), q - 96) for q in (128, 160) for h in (0, 4)
)
GROUPS = ((0, tuple(range(0, 8))), (32, (8, 9)), (64, (10, 11)))


def dot(a, b, over, precision=None):
    return lax.dot_general(a, b, ((over[:1], over[1:]), ((), ())), precision=precision, preferred_element_type=F32)


def take(ref, unit):
    q, n, heads, _ = unit
    parts = [ref[q : q + n, h * HEAD : (h + 1) * HEAD] for h in heads]
    return parts[0] if len(parts) == 1 else jnp.concatenate(parts, axis=0)


def put(ref, unit, value):
    q, n, heads, _ = unit
    for i, h in enumerate(heads):
        ref[q : q + n, h * HEAD : (h + 1) * HEAD] = value[i * n : (i + 1) * n]


def as_row(columns):
    return dot(jnp.ones((8, HEAD), F32), columns, (1, 1), lax.Precision.HIGHEST)[0:1]


def as_columns(row):
    eight = jnp.broadcast_to(row, (8, SEQ))
    return dot(eight, jnp.full((8, HEAD), 0.125, F32), (0, 0), lax.Precision.HIGHEST)


def fold(wide):
    total = wide[:, 0:HEAD]
    for h in range(1, HEADS):
        total = total + wide[:, h * HEAD : (h + 1) * HEAD]
    return total


def masks_of(segment):
    counts = [jnp.sum(jnp.where(segment < v, 1.0, 0.0), axis=1, keepdims=True) for v in (1, 2, 3)]
    start = jnp.where(segment >= 3, counts[2], jnp.where(segment >= 2, counts[1], jnp.where(segment >= 1, counts[0], 0.0)))
    key = lax.broadcasted_iota(jnp.int32, (HEAD, HEAD), 0).astype(F32)
    lane = lax.broadcasted_iota(jnp.int32, (HEAD, HEAD), 1)
    masks = {}
    query = lane.astype(F32)
    masks[0] = (key <= query) & (key >= start[:, 0:HEAD])
    tail = jnp.broadcast_to(start[:, HEAD:SEQ], (8, SEQ - HEAD)).astype(BF16)
    place = lax.broadcasted_iota(jnp.int32, (SEQ - HEAD, HEAD), 0)
    lanes = lax.broadcasted_iota(jnp.int32, (SEQ - HEAD, HEAD), 1)
    for q in (128, 160):
        pick = jnp.where(place == lax.rem(lanes, 32) + (q - 128), 1.0, 0.0).astype(BF16)
        first = dot(tail, pick, (1, 0))[0:1]
        query = (lax.rem(lane, 32) + q).astype(F32)
        keys = key + (q - 96)
        masks[q] = (keys <= query) & (keys >= first)
    return masks


def normalized(ref, out, rows, scale, gain):
    q, n = rows
    for h in range(HEADS):
        at = slice(h * HEAD, (h + 1) * HEAD)
        out[q : q + n, at] = (ref[q : q + n, at].astype(F32) * scale[q : q + n] * gain[:, at]).astype(BF16)


def weights_of(unit, normed, keys, mask):
    koff = unit[3]
    scores = dot(keys[koff : koff + HEAD, 0:HEAD], take(normed, unit), (1, 1)) * SCALE
    scores = jnp.where(mask, scores, -jnp.inf)
    grown = jnp.exp(scores - jnp.max(scores, axis=0, keepdims=True))
    return grown * (1.0 / jnp.sum(grown, axis=0, keepdims=True))


def kernel(
    order, segments, xs, gs, ys, gain_ref, wk_hbm, wv_hbm,
    fwd_out, bwd_out,
    xin, gin, y, w, nx, ny, kvx, kvy, pt, pbt, dst, dkv, dn,
    stat, cstat, xstat, xstat_in,
    load_sem, xsend, xrecv, gsend, grecv, ssend, srecv, csend, crecv, tsend, trecv,
):
    s, t = lax.axis_index("section"), lax.axis_index("tensor")
    nxt, prv = (lax.rem(s + 1, SECTIONS), t), (lax.rem(s + SECTIONS - 1, SECTIONS), t)
    peers = [(s, lax.rem(t + d, TENSOR)) for d in range(1, TENSOR)]

    barrier = pltpu.get_barrier_semaphore()
    for device in [nxt, prv] + peers:
        pl.semaphore_signal(barrier, inc=1, device_id=device, device_id_type=MESH)
    loads = [
        pltpu.make_async_copy(ys, y, load_sem.at[0]),
        pltpu.make_async_copy(wk_hbm, w.at[:, 0:HEAD], load_sem.at[1]),
        pltpu.make_async_copy(wv_hbm, w.at[:, HEAD : 2 * HEAD], load_sem.at[2]),
        pltpu.make_async_copy(xs, nx, load_sem.at[3]),
    ]
    for load in loads:
        load.start()
    gain = gain_ref[...]
    forward = order[s].astype(F32)
    segment = segments[...].astype(F32)
    seg_f = segment[0:1] + forward * (segment[1:2] - segment[0:1])
    seg_b = segment[1:2] + forward * (segment[0:1] - segment[1:2])
    loads[0].wait()
    loads[3].wait()

    def squares(ref):
        total = None
        for h in range(HEADS):
            part = ref[:, h * HEAD : (h + 1) * HEAD].astype(F32)
            total = part * part if total is None else total + part * part
        return as_row(total)

    stat[t, 0:1, :] = squares(y)
    stat[t, 1:2, :] = squares(nx)

    pl.semaphore_wait(barrier, 2 + len(peers))

    def remote(src, dst, send, recv, device):
        return pltpu.make_async_remote_copy(
            src_ref=src, dst_ref=dst, send_sem=send, recv_sem=recv, device_id=device, device_id_type=MESH
        )

    def to_peers(box, send, recv):
        return [remote(box.at[t], box.at[t], send.at[d], recv.at[t], peers[d]) for d in range(TENSOR - 1)]

    def from_peers(box, send, recv):
        for d in range(TENSOR - 1):
            slot = lax.rem(t + d + 1, TENSOR)
            remote(box.at[slot], box.at[slot], send.at[d], recv.at[slot], peers[d]).wait_recv()

    stat_sends = to_peers(stat, ssend, srecv)
    for copy in stat_sends:
        copy.start()
    g_copies = [remote(gs.at[pl.ds(q, n)], gin.at[pl.ds(q, n)], gsend.at[i], grecv.at[i], prv) for i, (q, n) in enumerate(CHUNKS)]
    x_copies = [remote(xs.at[pl.ds(q, n)], xin.at[pl.ds(q, n)], xsend.at[i], xrecv.at[i], nxt) for i, (q, n) in enumerate(CHUNKS)]
    for copy in g_copies + x_copies:
        copy.start()

    masks_b = masks_of(seg_b)
    masks_f = masks_of(seg_f)
    loads[1].wait()
    loads[2].wait()

    from_peers(stat, ssend, srecv)
    totals = jnp.sum(stat[...], axis=0)
    xstat[...] = totals[1:2]
    x_total = remote(xstat, xstat_in, tsend, trecv, nxt)
    x_total.start()

    scale_row = lax.rsqrt(totals[0:1] / D + EPSILON)
    scale = as_columns(scale_row)
    normalized(y, ny, (0, SEQ), scale, gain)
    kvy[...] = dot(ny[...], w[...], (1, 0)).astype(BF16)
    for u, unit in enumerate(UNITS):
        p = weights_of(unit, ny, kvy, masks_b[unit[0]])
        pt[:, u * HEAD : (u + 1) * HEAD] = p
        pbt[:, u * HEAD : (u + 1) * HEAD] = p.astype(BF16)

    def backward(units):
        for u in units:
            unit, at = UNITS[u], slice(u * HEAD, (u + 1) * HEAD)
            koff = unit[3]
            dp = dot(kvy[koff : koff + HEAD, HEAD : 2 * HEAD], take(gin, unit), (1, 1))
            p = pt[:, at]
            rows = jnp.sum(dp * p, axis=0, keepdims=True)
            ds = (p * (dp - rows) * SCALE).astype(BF16)
            dst[:, at] = ds
            put(dn, unit, dot(ds, kvy[koff : koff + HEAD, 0:HEAD], (0, 0)))

    def key_grads(group):
        koff, units = group
        at = slice(units[0] * HEAD, (units[-1] + 1) * HEAD)
        grads = jnp.concatenate([take(gin, UNITS[u]) for u in units], axis=0)
        queries = jnp.concatenate([take(ny, UNITS[u]) for u in units], axis=0)
        dkv[koff : koff + HEAD, 0:HEAD] += dot(dst[:, at], queries, (1, 0))
        dkv[koff : koff + HEAD, HEAD : 2 * HEAD] += dot(pbt[:, at], grads, (1, 0))

    dkv[...] = jnp.zeros_like(dkv)
    g_copies[0].wait_recv()
    backward(GROUPS[0][1])
    key_grads(GROUPS[0])
    g_copies[1].wait_recv()
    for group in GROUPS[1:]:
        backward(group[1])
        key_grads(group)
    rounded = dkv[...].astype(BF16)
    total = None
    scale_b = scale
    for h in range(HEADS):
        at = slice(h * HEAD, (h + 1) * HEAD)
        d = dn[:, at] + dot(rounded, w[at, :], (1, 1))
        scaled = d * gain[:, at]
        dn[:, at] = gin[:, at].astype(F32) + scale_b * scaled
        part = scaled * y[:, at].astype(F32)
        total = part if total is None else total + part
    cstat[t, 0:1, :] = as_row(total)
    c_sends = to_peers(cstat, csend, crecv)
    for copy in c_sends:
        copy.start()

    for copy in x_copies:
        copy.wait_recv()
    x_total.wait_recv()
    scale_f = as_columns(lax.rsqrt(xstat_in[...] / D + EPSILON))
    normalized(xin, nx, (0, SEQ), scale_f, gain)
    kvx[...] = dot(nx[...], w[...], (1, 0)).astype(BF16)
    for unit in UNITS:
        koff = unit[3]
        p = weights_of(unit, nx, kvx, masks_f[unit[0]]).astype(BF16)
        mixed = dot(p, kvx[koff : koff + HEAD, HEAD : 2 * HEAD], (0, 0)).astype(BF16).astype(F32)
        put(fwd_out, unit, (take(xin, unit).astype(F32) + mixed).astype(BF16))

    from_peers(cstat, csend, crecv)
    inner = jnp.sum(cstat[...], axis=0)
    pull = as_columns(scale_row * scale_row * scale_row / D * inner)
    for h in range(HEADS):
        at = slice(h * HEAD, (h + 1) * HEAD)
        bwd_out[:, at] = (dn[:, at] - y[:, at].astype(F32) * pull).astype(BF16)

    for copy in stat_sends + g_copies + x_copies + [x_total] + c_sends:
        copy.wait_send()


def on_device(produced, saved_inputs, upstream, norm_gain, w_key, w_value, batch_order, segment_ids):
    section = lax.axis_index("section")
    wanted = lax.dynamic_index_in_dim(batch_order, lax.rem(section + 1, SECTIONS), 0, keepdims=False)
    sent = lax.dynamic_index_in_dim(produced[0], wanted, 0, keepdims=False)
    rows = jax.ShapeDtypeStruct((SEQ, WIDTH), BF16)
    hbm, vmem = pl.BlockSpec(memory_space=pl.ANY), pl.BlockSpec(memory_space=pltpu.VMEM)
    stream = pltpu.VMEM((SEQ, WIDTH), BF16)
    wide = len(UNITS) * HEAD
    dma = pltpu.SemaphoreType.DMA
    forward_out, input_grad = pl.pallas_call(
        kernel,
        out_shape=(rows, rows),
        in_specs=[pl.BlockSpec(memory_space=pltpu.SMEM), vmem, hbm, hbm, hbm, vmem, hbm, hbm],
        out_specs=(vmem, vmem),
        scratch_shapes=[
            stream, stream, stream,
            pltpu.VMEM((WIDTH, 2 * HEAD), BF16),
            stream, stream,
            pltpu.VMEM((SEQ, 2 * HEAD), BF16), pltpu.VMEM((SEQ, 2 * HEAD), BF16),
            pltpu.VMEM((HEAD, wide), F32), pltpu.VMEM((HEAD, wide), BF16), pltpu.VMEM((HEAD, wide), BF16),
            pltpu.VMEM((SEQ, 2 * HEAD), F32), pltpu.VMEM((SEQ, WIDTH), F32),
            pltpu.VMEM((TENSOR, 2, SEQ), F32), pltpu.VMEM((TENSOR, 1, SEQ), F32),
            pltpu.VMEM((1, SEQ), F32), pltpu.VMEM((1, SEQ), F32),
            dma((4,)), dma((len(CHUNKS),)), dma((len(CHUNKS),)), dma((len(CHUNKS),)), dma((len(CHUNKS),)),
            dma((TENSOR - 1,)), dma((TENSOR,)), dma((TENSOR - 1,)), dma((TENSOR,)), dma, dma,
        ],
        compiler_params=pltpu.CompilerParams(collective_id=0, has_side_effects=True),
    )(batch_order, segment_ids, sent, upstream[0], saved_inputs[0], norm_gain, w_key[0, 0], w_value[0, 0])
    return forward_out[None], input_grad[None]


def solution(mesh):
    return jax.shard_map(
        on_device,
        mesh=mesh,
        in_specs=(
            P("section", None, None, "tensor"),
            P("section", None, "tensor"),
            P("section", None, "tensor"),
            P("section", "tensor"),
            P("section", "tensor", None, None),
            P("section", "tensor", None, None),
            P(),
            P(),
        ),
        out_specs=(P("section", None, "tensor"), P("section", None, "tensor")),
        check_vma=False,
    )
```

time: 107 us -> 60.9 us (0.57)
  Pallas kernels: 0 us -> 53.4 us
  blocking collectives: 53.1 us -> 0 us
  starting transfers between devices: 23.2 us -> 0 us
  matrix products: 11.4 us -> 0 us
  other arithmetic: 10.2 us -> 0 us
  between operations: 4.12 us -> 2.62 us
    pallas_call x0 -> x1, Pallas kernels: none -> 53.4 us  [on_device(): pl.pallas_call(kernel, out_shape=(rows, rows), in_specs=[pl.BlockSpec(mem...]
    psum x2 -> x0, blocking collectives: 53.1 us -> none  [on_device(): lax.psum((jnp.sum(forward_wide * forward_wide, axis=-1), jnp.sum(backward...]
    ppermute x2 -> x0, starting transfers between devices: 23.2 us -> none  [from_behind(): return lax.ppermute(block, axis, route)]
    dot_general x8 -> x0, matrix products: 11.4 us -> none  [the longest x1 2.59 us: on_device(): jnp.einsum('kglm,mkd->lkgd', rounded, value_rows, preferred_element_type=...]
    reduce_sum x4 -> x0, other arithmetic: 2.82 us -> none  [the longest x1 1.16 us: on_device(): jnp.sum(forward_wide * forward_wide, axis=-1)]
    unnamed x3 -> x0, other arithmetic: 2.41 us -> none
    unnamed x19 -> x8, local copies, waits for them, and re-layouts: 1.21 us -> 3.3 us
    convert_element_type x1 -> x0, other arithmetic: 1.96 us -> none  [on_device(): forward_rows = (forward_wide + mixed_heads.reshape(forward_in.shape).asty...]
  transfers between devices with their start and end apart: 2 -> 0, of which waited for: 0 -> 0; matrix products, arithmetic and copies ran while one was open for 14% -> 0% of each run, Pallas kernels for 0% -> 0%
where the time goes in v1:
time: 60.9 us; the launch traced here: 60.7 us
  Pallas kernels  53.4 us (88%)
  local copies, waits for them, and re-layouts  4.66 us (8%)
  between operations  2.62 us (4%)
    pallas_call x1, Pallas kernels, on_device(): pl.pallas_call(kernel, out_shape=(rows, rows), in_specs=[pl.BlockSpec(mem...  53.4 us
    unnamed x8, local copies, waits for them, and re-layouts  3.3 us

profile of v1, /device:TPU:1, one launch (start us, length us, event | category | flops | bytes accessed | tf_op | source)
XLA Modules:
  0.0 60.7 jit_solution(13420256917804293640)
XLA Ops:
  0.6 0.0 copy-start
  0.7 0.0 copy-start.2
  0.7 0.7 %copy-done.2 = s32[128]{0:T(128)S(1)} copy-done((s32[128]{0:T(128)S(1)}, s32[128]{0:T(128)}, u32[]{:S(2)}) %copy-start.2) | copy-done | bytes 536
  1.4 0.6 dynamic_slice.8
  3.9 0.0 copy-done
  3.9 0.8 %dynamic-slice_bitcast_fusion.xs = bf16[192,1024]{1,0:T(8,128)(2,1)} fusion(bf16[1,2,192,1024]{3,2,1,0:T(8,128)(2,1)S(1)} %copy-done, s32[]{:T(128)S(6)} %select_n.9), kind=kLoop, calls=%fused_computation | loop fusion | bytes 786436 | tf_op jit(solution)/shard_map/jit(dynamic_index_in_dim)/squeeze | solution.py:241
  4.7 53.4 %shard_map.95 = (bf16[192,1024]{1,0:T(8,128)(2,1)}, bf16[192,1024]{1,0:T(8,128)(2,1)}) custom-call(s32[128]{0:T(128)} %order.1, s32[2,192]{1,0:T(2,128)} %segments.1, bf16[192,1024]{1,0:T(8,128)(2,1)} %dynamic-slice_bitcast_fusion.xs, bf16[192,1024]{1,0:T(8,128)(2,1)} %bitcast.11, bf16[192,1024]{1,0:T(8,128)(2,1)} %bitcast.12, f32[1,1024]{1,0:T(1,128)} %gain_ref.1, ...), custom_call_target="tpu_custom_call" | custom-call | tf_op jit(solution)/shard_map/pallas_call | solution.py:247
  58.1 0.0 copy-start.1
  58.1 1.8 %copy.12 = bf16[1,192,1024]{2,1,0:T(8,128)(2,1)} copy(bf16[1,192,1024]{2,1,0:T(8,128)(2,1)} %bitcast.10) | data formatting | bytes 786432
  59.9 0.0 copy-done.1
  59.9 0.7 %copy.13 = bf16[1,192,1024]{2,1,0:T(8,128)(2,1)} copy(bf16[1,192,1024]{2,1,0:T(8,128)(2,1)S(1)} %bitcast.9) | data formatting | bytes 786432
Async XLA Ops:
  0.6 3.3 %copy-start = (bf16[1,2,192,1024]{3,2,1,0:T(8,128)(2,1)S(1)}, bf16[1,2,192,1024]{3,2,1,0:T(8,128)(2,1)}, u32[]{:S(2)}) copy-start(bf16[1,2,192,1024]{3,2,1,0:T(8,128)(2,1)} %param.8) | copy-start | bytes 2359300
  0.7 0.7 %copy-start.2 = (s32[128]{0:T(128)S(1)}, s32[128]{0:T(128)}, u32[]{:S(2)}) copy-start(s32[128]{0:T(128)} %order.1) | copy-start | bytes 1540
  58.1 1.8 %copy-start.1 = (bf16[192,1024]{1,0:T(8,128)(2,1)S(1)}, bf16[192,1024]{1,0:T(8,128)(2,1)}, u32[]{:S(2)}) copy-start(bf16[192,1024]{1,0:T(8,128)(2,1)} %get-tuple-element.5) | copy-start | bytes 1179652

commit v2 on v1

--- a/solution.py
+++ b/solution.py
@@ -88,34 +88,69 @@
 
 
 def kernel(
-    order, segments, xs, gs, ys, gain_ref, wk_hbm, wv_hbm,
+    order_hbm, segments_hbm, produced, gs, ys, gain_hbm, wk_hbm, wv_hbm,
     fwd_out, bwd_out,
-    xin, gin, y, w, nx, ny, kvx, kvy, pt, pbt, dst, dkv, dn,
+    order, segments, gain_ref, pair, xs, xin, gin, y, w, nx, ny, kvx, kvy, pt, pbt, dst, dkv, dn,
     stat, cstat, xstat, xstat_in,
     load_sem, xsend, xrecv, gsend, grecv, ssend, srecv, csend, crecv, tsend, trecv,
+    peer_in, next_in, previous_in,
 ):
     s, t = lax.axis_index("section"), lax.axis_index("tensor")
     nxt, prv = (lax.rem(s + 1, SECTIONS), t), (lax.rem(s + SECTIONS - 1, SECTIONS), t)
     peers = [(s, lax.rem(t + d, TENSOR)) for d in range(1, TENSOR)]
+    place = lax.rem(s, 16)
+
+    def signal(semaphore, device):
+        pl.semaphore_signal(semaphore, inc=1, device_id=device, device_id_type=MESH)
 
     barrier = pltpu.get_barrier_semaphore()
-    for device in [nxt, prv] + peers:
-        pl.semaphore_signal(barrier, inc=1, device_id=device, device_id_type=MESH)
+    for d in range(TENSOR - 1):
+        pl.when(t + d + 1 < TENSOR)(lambda d=d: signal(barrier, peers[d]))
+    pl.when(place != 15)(lambda: signal(barrier, nxt))
+    pl.when(place == 0)(lambda: signal(barrier, prv))
     loads = [
-        pltpu.make_async_copy(ys, y, load_sem.at[0]),
-        pltpu.make_async_copy(wk_hbm, w.at[:, 0:HEAD], load_sem.at[1]),
-        pltpu.make_async_copy(wv_hbm, w.at[:, HEAD : 2 * HEAD], load_sem.at[2]),
-        pltpu.make_async_copy(xs, nx, load_sem.at[3]),
+        pltpu.make_async_copy(produced, pair, load_sem.at[0]),
+        pltpu.make_async_copy(order_hbm, order, load_sem.at[1]),
+        pltpu.make_async_copy(ys, y, load_sem.at[2]),
+        pltpu.make_async_copy(wk_hbm, w.at[:, 0:HEAD], load_sem.at[3]),
+        pltpu.make_async_copy(wv_hbm, w.at[:, HEAD : 2 * HEAD], load_sem.at[4]),
+        pltpu.make_async_copy(segments_hbm, segments, load_sem.at[5]),
+        pltpu.make_async_copy(gain_hbm, gain_ref, load_sem.at[6]),
     ]
     for load in loads:
         load.start()
-    gain = gain_ref[...]
-    forward = order[s].astype(F32)
-    segment = segments[...].astype(F32)
-    seg_f = segment[0:1] + forward * (segment[1:2] - segment[0:1])
-    seg_b = segment[1:2] + forward * (segment[0:1] - segment[1:2])
+    greeted = t + jnp.where(place != 0, 1, 0) + jnp.where(place == 15, 1, 0)
+    pl.when(greeted > 0)(lambda: pl.semaphore_wait(barrier, greeted))
+    pl.when(place != 0)(lambda: signal(next_in, prv))
+    pl.when(place == 15)(lambda: signal(previous_in, nxt))
+    for d in range(TENSOR - 1):
+        pl.when(t + d + 1 >= TENSOR)(lambda d=d: signal(peer_in, peers[d]))
+
+    def remote(src, dst, send, recv, device):
+        return pltpu.make_async_remote_copy(
+            src_ref=src, dst_ref=dst, send_sem=send, recv_sem=recv, device_id=device, device_id_type=MESH
+        )
+
+    g_copies = [remote(gs.at[pl.ds(q, n)], gin.at[pl.ds(q, n)], gsend.at[i], grecv.at[i], prv) for i, (q, n) in enumerate(CHUNKS)]
+    x_copies = [remote(xs.at[pl.ds(q, n)], xin.at[pl.ds(q, n)], xsend.at[i], xrecv.at[i], nxt) for i, (q, n) in enumerate(CHUNKS)]
+    x_total = remote(xstat, xstat_in, tsend, trecv, nxt)
+
+    @pl.when(place != 0)
+    def _():
+        for copy in g_copies:
+            copy.start()
+
     loads[0].wait()
-    loads[3].wait()
+    loads[1].wait()
+    wanted = order[lax.rem(s + 1, SECTIONS)]
+    xs[...] = pair[wanted]
+
+    @pl.when(place != 7)
+    def _():
+        pl.when(place != 15)(lambda: pl.semaphore_wait(next_in, 1))
+        x_copies[0].start()
+
+    loads[2].wait()
 
     def squares(ref):
         total = None
@@ -125,14 +160,7 @@
         return as_row(total)
 
     stat[t, 0:1, :] = squares(y)
-    stat[t, 1:2, :] = squares(nx)
-
-    pl.semaphore_wait(barrier, 2 + len(peers))
-
-    def remote(src, dst, send, recv, device):
-        return pltpu.make_async_remote_copy(
-            src_ref=src, dst_ref=dst, send_sem=send, recv_sem=recv, device_id=device, device_id_type=MESH
-        )
+    stat[t, 1:2, :] = squares(xs)
 
     def to_peers(box, send, recv):
         return [remote(box.at[t], box.at[t], send.at[d], recv.at[t], peers[d]) for d in range(TENSOR - 1)]
@@ -142,24 +170,27 @@
             slot = lax.rem(t + d + 1, TENSOR)
             remote(box.at[slot], box.at[slot], send.at[d], recv.at[slot], peers[d]).wait_recv()
 
+    pl.when(t < TENSOR - 1)(lambda: pl.semaphore_wait(peer_in, TENSOR - 1 - t))
     stat_sends = to_peers(stat, ssend, srecv)
     for copy in stat_sends:
         copy.start()
-    g_copies = [remote(gs.at[pl.ds(q, n)], gin.at[pl.ds(q, n)], gsend.at[i], grecv.at[i], prv) for i, (q, n) in enumerate(CHUNKS)]
-    x_copies = [remote(xs.at[pl.ds(q, n)], xin.at[pl.ds(q, n)], xsend.at[i], xrecv.at[i], nxt) for i, (q, n) in enumerate(CHUNKS)]
-    for copy in g_copies + x_copies:
-        copy.start()
-
-    masks_b = masks_of(seg_b)
-    masks_f = masks_of(seg_f)
-    loads[1].wait()
-    loads[2].wait()
+
+    for load in loads[3:]:
+        load.wait()
+    gain = gain_ref[...]
+    forward = order[s].astype(F32)
+    segment = segments[...].astype(F32)
+    masks_b = masks_of(segment[1:2] + forward * (segment[0:1] - segment[1:2]))
+    masks_f = masks_of(segment[0:1] + forward * (segment[1:2] - segment[0:1]))
 
     from_peers(stat, ssend, srecv)
     totals = jnp.sum(stat[...], axis=0)
     xstat[...] = totals[1:2]
-    x_total = remote(xstat, xstat_in, tsend, trecv, nxt)
-    x_total.start()
+
+    @pl.when(place != 7)
+    def _():
+        x_total.start()
+        x_copies[1].start()
 
     scale_row = lax.rsqrt(totals[0:1] / D + EPSILON)
     scale = as_columns(scale_row)
@@ -169,6 +200,18 @@
         p = weights_of(unit, ny, kvy, masks_b[unit[0]])
         pt[:, u * HEAD : (u + 1) * HEAD] = p
         pbt[:, u * HEAD : (u + 1) * HEAD] = p.astype(BF16)
+
+    @pl.when(place == 0)
+    def _():
+        pl.semaphore_wait(previous_in, 1)
+        for copy in g_copies:
+            copy.start()
+
+    @pl.when(place == 7)
+    def _():
+        pl.semaphore_wait(next_in, 1)
+        for copy in (x_total, *x_copies):
+            copy.start()
 
     def backward(units):
         for u in units:
@@ -199,12 +242,11 @@
         key_grads(group)
     rounded = dkv[...].astype(BF16)
     total = None
-    scale_b = scale
     for h in range(HEADS):
         at = slice(h * HEAD, (h + 1) * HEAD)
         d = dn[:, at] + dot(rounded, w[at, :], (1, 1))
         scaled = d * gain[:, at]
-        dn[:, at] = gin[:, at].astype(F32) + scale_b * scaled
+        dn[:, at] = gin[:, at].astype(F32) + scale * scaled
         part = scaled * y[:, at].astype(F32)
         total = part if total is None else total + part
     cstat[t, 0:1, :] = as_row(total)
@@ -212,45 +254,62 @@
     for copy in c_sends:
         copy.start()
 
-    for copy in x_copies:
-        copy.wait_recv()
+    def finish_backward():
+        from_peers(cstat, csend, crecv)
+        inner = jnp.sum(cstat[...], axis=0)
+        pull = as_columns(scale_row * scale_row * scale_row / D * inner)
+        for h in range(HEADS):
+            at = slice(h * HEAD, (h + 1) * HEAD)
+            bwd_out[:, at] = (dn[:, at] - y[:, at].astype(F32) * pull).astype(BF16)
+
+    late_forward = lax.rem(s, 8) == 0
+    pl.when(late_forward)(finish_backward)
+
+    x_copies[0].wait_recv()
     x_total.wait_recv()
     scale_f = as_columns(lax.rsqrt(xstat_in[...] / D + EPSILON))
-    normalized(xin, nx, (0, SEQ), scale_f, gain)
-    kvx[...] = dot(nx[...], w[...], (1, 0)).astype(BF16)
-    for unit in UNITS:
-        koff = unit[3]
-        p = weights_of(unit, nx, kvx, masks_f[unit[0]]).astype(BF16)
-        mixed = dot(p, kvx[koff : koff + HEAD, HEAD : 2 * HEAD], (0, 0)).astype(BF16).astype(F32)
-        put(fwd_out, unit, (take(xin, unit).astype(F32) + mixed).astype(BF16))
-
-    from_peers(cstat, csend, crecv)
-    inner = jnp.sum(cstat[...], axis=0)
-    pull = as_columns(scale_row * scale_row * scale_row / D * inner)
-    for h in range(HEADS):
-        at = slice(h * HEAD, (h + 1) * HEAD)
-        bwd_out[:, at] = (dn[:, at] - y[:, at].astype(F32) * pull).astype(BF16)
+    for i, (q, n) in enumerate(CHUNKS):
+        if i:
+            x_copies[i].wait_recv()
+        normalized(xin, nx, (q, n), scale_f, gain)
+        kvx[q : q + n] = dot(nx[q : q + n], w[...], (1, 0)).astype(BF16)
+        for unit in UNITS:
+            if q <= unit[0] < q + n:
+                koff = unit[3]
+                p = weights_of(unit, nx, kvx, masks_f[unit[0]]).astype(BF16)
+                mixed = dot(p, kvx[koff : koff + HEAD, HEAD : 2 * HEAD], (0, 0)).astype(BF16).astype(F32)
+                put(fwd_out, unit, (take(xin, unit).astype(F32) + mixed).astype(BF16))
+
+    pl.when(jnp.logical_not(late_forward))(finish_backward)
 
     for copy in stat_sends + g_copies + x_copies + [x_total] + c_sends:
         copy.wait_send()
 
 
+def write_out(first, second, first_out, second_out, semaphore):
+    copies = [pltpu.make_async_copy(first, first_out, semaphore.at[0]), pltpu.make_async_copy(second, second_out, semaphore.at[1])]
+    for copy in copies:
+        copy.start()
+    for copy in copies:
+        copy.wait()
+
+
 def on_device(produced, saved_inputs, upstream, norm_gain, w_key, w_value, batch_order, segment_ids):
-    section = lax.axis_index("section")
-    wanted = lax.dynamic_index_in_dim(batch_order, lax.rem(section + 1, SECTIONS), 0, keepdims=False)
-    sent = lax.dynamic_index_in_dim(produced[0], wanted, 0, keepdims=False)
     rows = jax.ShapeDtypeStruct((SEQ, WIDTH), BF16)
-    hbm, vmem = pl.BlockSpec(memory_space=pl.ANY), pl.BlockSpec(memory_space=pltpu.VMEM)
+    hbm, vmem = pl.BlockSpec(memory_space=pltpu.HBM), pl.BlockSpec(memory_space=pltpu.VMEM)
     stream = pltpu.VMEM((SEQ, WIDTH), BF16)
     wide = len(UNITS) * HEAD
-    dma = pltpu.SemaphoreType.DMA
+    dma, regular = pltpu.SemaphoreType.DMA, pltpu.SemaphoreType.REGULAR
+    parts = len(CHUNKS)
     forward_out, input_grad = pl.pallas_call(
         kernel,
         out_shape=(rows, rows),
-        in_specs=[pl.BlockSpec(memory_space=pltpu.SMEM), vmem, hbm, hbm, hbm, vmem, hbm, hbm],
+        in_specs=[hbm] * 8,
         out_specs=(vmem, vmem),
         scratch_shapes=[
-            stream, stream, stream,
+            pltpu.SMEM((SECTIONS,), jnp.int32), pltpu.VMEM((2, SEQ), jnp.int32), pltpu.VMEM((1, WIDTH), F32),
+            pltpu.VMEM((2, SEQ, WIDTH), BF16),
+            stream, stream, stream, stream,
             pltpu.VMEM((WIDTH, 2 * HEAD), BF16),
             stream, stream,
             pltpu.VMEM((SEQ, 2 * HEAD), BF16), pltpu.VMEM((SEQ, 2 * HEAD), BF16),
@@ -258,11 +317,20 @@
             pltpu.VMEM((SEQ, 2 * HEAD), F32), pltpu.VMEM((SEQ, WIDTH), F32),
             pltpu.VMEM((TENSOR, 2, SEQ), F32), pltpu.VMEM((TENSOR, 1, SEQ), F32),
             pltpu.VMEM((1, SEQ), F32), pltpu.VMEM((1, SEQ), F32),
-            dma((4,)), dma((len(CHUNKS),)), dma((len(CHUNKS),)), dma((len(CHUNKS),)), dma((len(CHUNKS),)),
+            dma((7,)), dma((parts,)), dma((parts,)), dma((parts,)), dma((parts,)),
             dma((TENSOR - 1,)), dma((TENSOR,)), dma((TENSOR - 1,)), dma((TENSOR,)), dma, dma,
+            regular, regular, regular,
         ],
-        compiler_params=pltpu.CompilerParams(collective_id=0, has_side_effects=True),
-    )(batch_order, segment_ids, sent, upstream[0], saved_inputs[0], norm_gain, w_key[0, 0], w_value[0, 0])
+        compiler_params=pltpu.CompilerParams(collective_id=0, has_side_effects=True, vmem_limit_bytes=24 << 20),
+    )(*[pltpu.with_memory_space_constraint(a, pltpu.HBM) for a in (batch_order, segment_ids, produced[0], upstream[0], saved_inputs[0], norm_gain, w_key[0, 0], w_value[0, 0])])
+    forward_out, input_grad = pl.pallas_call(
+        write_out,
+        out_shape=(rows, rows),
+        in_specs=[vmem, vmem],
+        out_specs=(hbm, hbm),
+        scratch_shapes=[dma((2,))],
+        compiler_params=pltpu.CompilerParams(vmem_limit_bytes=4 << 20),
+    )(forward_out, input_grad)
     return forward_out[None], input_grad[None]
 
 

time: 60.9 us -> 53.3 us (0.88)
  local copies, waits for them, and re-layouts: 4.66 us -> 0 us
  between operations: 2.62 us -> 0.64 us
  Pallas kernels: 53.4 us -> 52.5 us
    unnamed x8 -> x0, local copies, waits for them, and re-layouts: 3.3 us -> none
    pallas_call x1 -> x2, Pallas kernels: 53.4 us -> 52.5 us  [the longest x1 51.6 us: on_device(): pl.pallas_call(kernel, out_shape=(rows, rows), in_specs=[hbm] * 8, out_sp...]
    squeeze x1 -> x0, local copies, waits for them, and re-layouts: 0.78 us -> none  [on_device(): sent = lax.dynamic_index_in_dim(produced[0], wanted, 0, keepdims=False)]
where the time goes in v2:
time: 53.3 us; the launch traced here: 53.1 us
  Pallas kernels  52.5 us (98%)
  between operations  0.64 us (1%)
    pallas_call x1, Pallas kernels, on_device(): pl.pallas_call(kernel, out_shape=(rows, rows), in_specs=[hbm] * 8, out_sp...  51.6 us

profile of v2, /device:TPU:1, one launch (start us, length us, event | category | flops | bytes accessed | tf_op | source)
XLA Modules:
  0.0 53.1 jit_solution(5770130420085025399)
XLA Ops:
  0.6 51.6 %shard_map.95 = (bf16[192,1024]{1,0:T(8,128)(2,1)S(1)}, bf16[192,1024]{1,0:T(8,128)(2,1)S(1)}) custom-call(s32[128]{0:T(128)} %order_hbm.1, s32[2,192]{1,0:T(2,128)} %segments_hbm.1, bf16[2,192,1024]{2,1,0:T(8,128)(2,1)} %bitcast.7, bf16[192,1024]{1,0:T(8,128)(2,1)} %bitcast.8, bf16[192,1024]{1,0:T(8,128)(2,1)} %bitcast.9, f32[1,1024]{1,0:T(1,128)} %gain_hbm.1, ...), custom_call_target="tpu_custom_call" | custom-call | tf_op jit(solution)/shard_map/pallas_call | solution.py:304
  52.2 0.9 %shard_map.96 = (bf16[192,1024]{1,0:T(8,128)(2,1)}, bf16[192,1024]{1,0:T(8,128)(2,1)}) custom-call(bf16[192,1024]{1,0:T(8,128)(2,1)S(1)} %get-tuple-element.6.first, bf16[192,1024]{1,0:T(8,128)(2,1)S(1)} %get-tuple-element.7.second), custom_call_target="tpu_custom_call" | custom-call | tf_op jit(solution)/shard_map/pallas_call | solution.py:326

commit v3 on v2

--- a/solution.py
+++ b/solution.py
@@ -13,6 +13,9 @@
 MESH = pl.DeviceIdType.MESH
 F32, BF16 = jnp.float32, jnp.bfloat16
 CHUNKS = ((0, 128), (128, 64))
+PIECES = tuple((i * 32, 32) for i in range(4)) + tuple((128 + i * 16, 16) for i in range(4))
+HELD = ((0, 32), (32, 16))
+X_RELAYS, G_RELAYS = (7, 6, 1), (0, 1, 6)
 
 UNITS = tuple((0, 128, (h,), 0) for h in range(HEADS)) + tuple(
     (q, 32, tuple(range(h, h + 4)), q - 96) for q in (128, 160) for h in (0, 4)
@@ -93,12 +96,26 @@
     order, segments, gain_ref, pair, xs, xin, gin, y, w, nx, ny, kvx, kvy, pt, pbt, dst, dkv, dn,
     stat, cstat, xstat, xstat_in,
     load_sem, xsend, xrecv, gsend, grecv, ssend, srecv, csend, crecv, tsend, trecv,
-    peer_in, next_in, previous_in,
+    peer_in, next_in, previous_in, x_relay_in, g_relay_in,
+    x_held, g_held, x_held_recv, g_held_recv, x_held_send, g_held_send,
 ):
     s, t = lax.axis_index("section"), lax.axis_index("tensor")
     nxt, prv = (lax.rem(s + 1, SECTIONS), t), (lax.rem(s + SECTIONS - 1, SECTIONS), t)
     peers = [(s, lax.rem(t + d, TENSOR)) for d in range(1, TENSOR)]
     place = lax.rem(s, 16)
+    x, block = lax.rem(s, 8), s // 8
+    late = lax.rem(block, 2) == 1
+
+    def partner(b):
+        return b + 1 - 2 * lax.rem(b, 2)
+
+    def relays(b, columns):
+        return [(partner(b) * 8 + column, t) for column in columns]
+
+    x_path = jnp.where(x == 7, 1, jnp.where(x == 6, 2, jnp.where(x == 1, 3, 0)))
+    g_path = jnp.where(x == 0, 1, jnp.where(x == 1, 2, jnp.where(x == 6, 3, 0)))
+    x_source, x_target = (partner(block) * 8 + 7, t), (lax.rem(partner(block) * 8 + 8, SECTIONS), t)
+    g_source, g_target = (partner(block) * 8, t), (lax.rem(partner(block) * 8 + SECTIONS - 1, SECTIONS), t)
 
     def signal(semaphore, device):
         pl.semaphore_signal(semaphore, inc=1, device_id=device, device_id_type=MESH)
@@ -108,6 +125,17 @@
         pl.when(t + d + 1 < TENSOR)(lambda d=d: signal(barrier, peers[d]))
     pl.when(place != 15)(lambda: signal(barrier, nxt))
     pl.when(place == 0)(lambda: signal(barrier, prv))
+
+    def greet(devices):
+        for device in devices:
+            signal(barrier, device)
+
+    pl.when((x_path > 0) & jnp.logical_not(late))(lambda: greet([x_source]))
+    pl.when((g_path > 0) & jnp.logical_not(late))(lambda: greet([g_source]))
+    pl.when(place == 7)(lambda: greet(relays(block, X_RELAYS)))
+    pl.when(place == 0)(lambda: greet(relays(block, G_RELAYS)))
+    pl.when(x == 0)(lambda: greet(relays(lax.rem(s + SECTIONS - 1, SECTIONS) // 8, X_RELAYS)))
+    pl.when(x == 7)(lambda: greet(relays(lax.rem(s + 1, SECTIONS) // 8, G_RELAYS)))
     loads = [
         pltpu.make_async_copy(produced, pair, load_sem.at[0]),
         pltpu.make_async_copy(order_hbm, order, load_sem.at[1]),
@@ -119,10 +147,16 @@
     ]
     for load in loads:
         load.start()
-    greeted = t + jnp.where(place != 0, 1, 0) + jnp.where(place == 15, 1, 0)
+    roles = jnp.where(x_path > 0, 1, 0) + jnp.where(g_path > 0, 1, 0)
+    greeted = (
+        t + jnp.where(place != 0, 1, 0) + jnp.where(place == 15, 4, 0) + jnp.where(place == 8, 3, 0)
+        + roles + jnp.where(late, roles, 0)
+    )
     pl.when(greeted > 0)(lambda: pl.semaphore_wait(barrier, greeted))
     pl.when(place != 0)(lambda: signal(next_in, prv))
     pl.when(place == 15)(lambda: signal(previous_in, nxt))
+    pl.when((x_path > 0) & late)(lambda: signal(x_relay_in, x_source))
+    pl.when((g_path > 0) & late)(lambda: signal(g_relay_in, g_source))
     for d in range(TENSOR - 1):
         pl.when(t + d + 1 >= TENSOR)(lambda d=d: signal(peer_in, peers[d]))
 
@@ -131,24 +165,55 @@
             src_ref=src, dst_ref=dst, send_sem=send, recv_sem=recv, device_id=device, device_id_type=MESH
         )
 
-    g_copies = [remote(gs.at[pl.ds(q, n)], gin.at[pl.ds(q, n)], gsend.at[i], grecv.at[i], prv) for i, (q, n) in enumerate(CHUNKS)]
-    x_copies = [remote(xs.at[pl.ds(q, n)], xin.at[pl.ds(q, n)], xsend.at[i], xrecv.at[i], nxt) for i, (q, n) in enumerate(CHUNKS)]
+    def straight(i, src, dst, send, recv, device):
+        q, n = PIECES[i]
+        return remote(src.at[pl.ds(q, n)], dst.at[pl.ds(q, n)], send.at[i], recv.at[i], device)
+
+    def to_relay(i, src, held, send, recv, device):
+        (q, n), (at, _) = PIECES[i], HELD[i // 4]
+        return remote(src.at[pl.ds(q, n)], held.at[pl.ds(at, n)], send.at[i], recv.at[i // 4], device)
+
+    def from_relay(j, path, held, dst, send, recv, device):
+        at, n = HELD[j]
+        rows = pl.ds(pl.multiple_of(128 * j + path * n, 16), n)
+        return remote(held.at[pl.ds(at, n)], dst.at[rows], send.at[j], recv.at[4 * j + path], device)
+
+    g_copies = [straight(i, gs, gin, gsend, grecv, prv) for i in range(8)]
+    x_copies = [straight(i, xs, xin, xsend, xrecv, nxt) for i in range(8)]
+    g_devices, x_devices = relays(block, G_RELAYS), relays(block, X_RELAYS)
+    g_split = [g_copies[i] if i % 4 == 0 else to_relay(i, gs, g_held, gsend, g_held_recv, g_devices[i % 4 - 1]) for i in range(8)]
+    x_split = [x_copies[i] if i % 4 == 0 else to_relay(i, xs, x_held, xsend, x_held_recv, x_devices[i % 4 - 1]) for i in range(8)]
     x_total = remote(xstat, xstat_in, tsend, trecv, nxt)
 
-    @pl.when(place != 0)
-    def _():
-        for copy in g_copies:
+    def start(copies):
+        for copy in copies:
             copy.start()
+
+    pl.when((x != 0) & (place != 15))(lambda: start(g_copies))
+    pl.when(place == 8)(lambda: start(g_split))
+
+    def serve(j):
+        def one(path, held, held_recv, held_send, dst, recv, target):
+            @pl.when(path > 0)
+            def _():
+                at, n = HELD[j]
+                remote(held.at[pl.ds(at, n)], held.at[pl.ds(at, n)], held_send.at[j], held_recv.at[j], target).wait_recv()
+                from_relay(j, path, held, dst, held_send, recv, target).start()
+
+        one(g_path, g_held, g_held_recv, g_held_send, gin, grecv, g_target)
+        one(x_path, x_held, x_held_recv, x_held_send, xin, xrecv, x_target)
 
     loads[0].wait()
     loads[1].wait()
     wanted = order[lax.rem(s + 1, SECTIONS)]
     xs[...] = pair[wanted]
 
-    @pl.when(place != 7)
+    pl.when(place == 15)(lambda: start(x_split[:4]))
+
+    @pl.when(x != 7)
     def _():
-        pl.when(place != 15)(lambda: pl.semaphore_wait(next_in, 1))
-        x_copies[0].start()
+        pl.semaphore_wait(next_in, 1)
+        start(x_copies[:4])
 
     loads[2].wait()
 
@@ -172,8 +237,7 @@
 
     pl.when(t < TENSOR - 1)(lambda: pl.semaphore_wait(peer_in, TENSOR - 1 - t))
     stat_sends = to_peers(stat, ssend, srecv)
-    for copy in stat_sends:
-        copy.start()
+    start(stat_sends)
 
     for load in loads[3:]:
         load.wait()
@@ -187,10 +251,8 @@
     totals = jnp.sum(stat[...], axis=0)
     xstat[...] = totals[1:2]
 
-    @pl.when(place != 7)
-    def _():
-        x_total.start()
-        x_copies[1].start()
+    pl.when(x != 7)(lambda: start([x_total] + x_copies[4:]))
+    pl.when(place == 15)(lambda: start([x_total] + x_split[4:] + g_copies))
 
     scale_row = lax.rsqrt(totals[0:1] / D + EPSILON)
     scale = as_columns(scale_row)
@@ -204,14 +266,14 @@
     @pl.when(place == 0)
     def _():
         pl.semaphore_wait(previous_in, 1)
-        for copy in g_copies:
-            copy.start()
+        pl.semaphore_wait(g_relay_in, 3)
+        start(g_split)
 
     @pl.when(place == 7)
     def _():
         pl.semaphore_wait(next_in, 1)
-        for copy in (x_total, *x_copies):
-            copy.start()
+        pl.semaphore_wait(x_relay_in, 3)
+        start([x_total] + x_split)
 
     def backward(units):
         for u in units:
@@ -233,10 +295,14 @@
         dkv[koff : koff + HEAD, HEAD : 2 * HEAD] += dot(pbt[:, at], grads, (1, 0))
 
     dkv[...] = jnp.zeros_like(dkv)
-    g_copies[0].wait_recv()
+    serve(0)
+    for copy in g_copies[:4]:
+        copy.wait_recv()
     backward(GROUPS[0][1])
     key_grads(GROUPS[0])
-    g_copies[1].wait_recv()
+    pl.when(x == 7)(lambda: serve(1))
+    for copy in g_copies[4:]:
+        copy.wait_recv()
     for group in GROUPS[1:]:
         backward(group[1])
         key_grads(group)
@@ -251,8 +317,8 @@
         total = part if total is None else total + part
     cstat[t, 0:1, :] = as_row(total)
     c_sends = to_peers(cstat, csend, crecv)
-    for copy in c_sends:
-        copy.start()
+    start(c_sends)
+    pl.when(x != 7)(lambda: serve(1))
 
     def finish_backward():
         from_peers(cstat, csend, crecv)
@@ -262,15 +328,16 @@
             at = slice(h * HEAD, (h + 1) * HEAD)
             bwd_out[:, at] = (dn[:, at] - y[:, at].astype(F32) * pull).astype(BF16)
 
-    late_forward = lax.rem(s, 8) == 0
-    pl.when(late_forward)(finish_backward)
-
-    x_copies[0].wait_recv()
+    pl.when(x == 0)(finish_backward)
+
+    for copy in x_copies[:4]:
+        copy.wait_recv()
     x_total.wait_recv()
     scale_f = as_columns(lax.rsqrt(xstat_in[...] / D + EPSILON))
     for i, (q, n) in enumerate(CHUNKS):
         if i:
-            x_copies[i].wait_recv()
+            for copy in x_copies[4:]:
+                copy.wait_recv()
         normalized(xin, nx, (q, n), scale_f, gain)
         kvx[q : q + n] = dot(nx[q : q + n], w[...], (1, 0)).astype(BF16)
         for unit in UNITS:
@@ -280,10 +347,19 @@
                 mixed = dot(p, kvx[koff : koff + HEAD, HEAD : 2 * HEAD], (0, 0)).astype(BF16).astype(F32)
                 put(fwd_out, unit, (take(xin, unit).astype(F32) + mixed).astype(BF16))
 
-    pl.when(jnp.logical_not(late_forward))(finish_backward)
+    pl.when(x != 0)(finish_backward)
 
     for copy in stat_sends + g_copies + x_copies + [x_total] + c_sends:
         copy.wait_send()
+    for path, held, held_send, dst, recv, target in (
+        (g_path, g_held, g_held_send, gin, grecv, g_target),
+        (x_path, x_held, x_held_send, xin, xrecv, x_target),
+    ):
+
+        @pl.when(path > 0)
+        def _(path=path, held=held, held_send=held_send, dst=dst, recv=recv, target=target):
+            for j in range(2):
+                from_relay(j, path, held, dst, held_send, recv, target).wait_send()
 
 
 def write_out(first, second, first_out, second_out, semaphore):
@@ -300,7 +376,8 @@
     stream = pltpu.VMEM((SEQ, WIDTH), BF16)
     wide = len(UNITS) * HEAD
     dma, regular = pltpu.SemaphoreType.DMA, pltpu.SemaphoreType.REGULAR
-    parts = len(CHUNKS)
+    parts = len(PIECES)
+    held = pltpu.VMEM((48, WIDTH), BF16)
     forward_out, input_grad = pl.pallas_call(
         kernel,
         out_shape=(rows, rows),
@@ -319,7 +396,8 @@
             pltpu.VMEM((1, SEQ), F32), pltpu.VMEM((1, SEQ), F32),
             dma((7,)), dma((parts,)), dma((parts,)), dma((parts,)), dma((parts,)),
             dma((TENSOR - 1,)), dma((TENSOR,)), dma((TENSOR - 1,)), dma((TENSOR,)), dma, dma,
-            regular, regular, regular,
+            regular, regular, regular, regular, regular,
+            held, held, dma((2,)), dma((2,)), dma((2,)), dma((2,)),
         ],
         compiler_params=pltpu.CompilerParams(collective_id=0, has_side_effects=True, vmem_limit_bytes=24 << 20),
     )(*[pltpu.with_memory_space_constraint(a, pltpu.HBM) for a in (batch_order, segment_ids, produced[0], upstream[0], saved_inputs[0], norm_gain, w_key[0, 0], w_value[0, 0])])

time: 53.3 us -> 46.6 us (0.87)
  Pallas kernels: 52.5 us -> 45.8 us
    pallas_call x1, Pallas kernels: 51.6 us -> 44.9 us  [on_device(): pl.pallas_call(kernel, out_shape=(rows, rows), in_specs=[hbm] * 8, out_sp...]
where the time goes in v3:
time: 46.6 us; the launch traced here: 46.4 us
  Pallas kernels  45.8 us (98%)
  between operations  0.64 us (1%)
    pallas_call x1, Pallas kernels, on_device(): pl.pallas_call(kernel, out_shape=(rows, rows), in_specs=[hbm] * 8, out_sp...  44.9 us

profile of v3, /device:TPU:1, one launch (start us, length us, event | category | flops | bytes accessed | tf_op | source)
XLA Modules:
  0.0 46.4 jit_solution(7209996266232812966)
XLA Ops:
  0.6 44.9 %shard_map.95 = (bf16[192,1024]{1,0:T(8,128)(2,1)S(1)}, bf16[192,1024]{1,0:T(8,128)(2,1)S(1)}) custom-call(s32[128]{0:T(128)} %order_hbm.1, s32[2,192]{1,0:T(2,128)} %segments_hbm.1, bf16[2,192,1024]{2,1,0:T(8,128)(2,1)} %bitcast.7, bf16[192,1024]{1,0:T(8,128)(2,1)} %bitcast.8, bf16[192,1024]{1,0:T(8,128)(2,1)} %bitcast.9, f32[1,1024]{1,0:T(1,128)} %gain_hbm.1, ...), custom_call_target="tpu_custom_call" | custom-call | tf_op jit(solution)/shard_map/pallas_call | solution.py:381
  45.5 0.9 %shard_map.96 = (bf16[192,1024]{1,0:T(8,128)(2,1)}, bf16[192,1024]{1,0:T(8,128)(2,1)}) custom-call(bf16[192,1024]{1,0:T(8,128)(2,1)S(1)} %get-tuple-element.6.first, bf16[192,1024]{1,0:T(8,128)(2,1)S(1)} %get-tuple-element.7.second), custom_call_target="tpu_custom_call" | custom-call | tf_op jit(solution)/shard_map/pallas_call | solution.py:404

commit v4 on v3

--- a/solution.py
+++ b/solution.py
@@ -40,12 +40,11 @@
 
 
 def as_row(columns):
-    return dot(jnp.ones((8, HEAD), F32), columns, (1, 1), lax.Precision.HIGHEST)[0:1]
+    return jnp.sum(jnp.transpose(columns), axis=0, keepdims=True)
 
 
 def as_columns(row):
-    eight = jnp.broadcast_to(row, (8, SEQ))
-    return dot(eight, jnp.full((8, HEAD), 0.125, F32), (0, 0), lax.Precision.HIGHEST)
+    return jnp.transpose(jnp.broadcast_to(row, (HEAD, SEQ)))
 
 
 def fold(wide):
@@ -96,7 +95,7 @@
     order, segments, gain_ref, pair, xs, xin, gin, y, w, nx, ny, kvx, kvy, pt, pbt, dst, dkv, dn,
     stat, cstat, xstat, xstat_in,
     load_sem, xsend, xrecv, gsend, grecv, ssend, srecv, csend, crecv, tsend, trecv,
-    peer_in, next_in, previous_in, x_relay_in, g_relay_in,
+    peer_in, next_in, previous_in, x_relay_in, g_relay_in, g_target_in,
     x_held, g_held, x_held_recv, g_held_recv, x_held_send, g_held_send,
 ):
     s, t = lax.axis_index("section"), lax.axis_index("tensor")
@@ -135,7 +134,7 @@
     pl.when(place == 7)(lambda: greet(relays(block, X_RELAYS)))
     pl.when(place == 0)(lambda: greet(relays(block, G_RELAYS)))
     pl.when(x == 0)(lambda: greet(relays(lax.rem(s + SECTIONS - 1, SECTIONS) // 8, X_RELAYS)))
-    pl.when(x == 7)(lambda: greet(relays(lax.rem(s + 1, SECTIONS) // 8, G_RELAYS)))
+    pl.when(g_path > 0)(lambda: greet([g_target]))
     loads = [
         pltpu.make_async_copy(produced, pair, load_sem.at[0]),
         pltpu.make_async_copy(order_hbm, order, load_sem.at[1]),
@@ -147,14 +146,20 @@
     ]
     for load in loads:
         load.start()
-    roles = jnp.where(x_path > 0, 1, 0) + jnp.where(g_path > 0, 1, 0)
+    x_role, g_role = jnp.where(x_path > 0, 1, 0), jnp.where(g_path > 0, 1, 0)
     greeted = (
         t + jnp.where(place != 0, 1, 0) + jnp.where(place == 15, 4, 0) + jnp.where(place == 8, 3, 0)
-        + roles + jnp.where(late, roles, 0)
+        + jnp.where(x == 7, 3, 0) + x_role + jnp.where(late, x_role + g_role, 0)
     )
     pl.when(greeted > 0)(lambda: pl.semaphore_wait(barrier, greeted))
     pl.when(place != 0)(lambda: signal(next_in, prv))
     pl.when(place == 15)(lambda: signal(previous_in, nxt))
+
+    @pl.when(x == 7)
+    def _():
+        for device in relays(lax.rem(s + 1, SECTIONS) // 8, G_RELAYS):
+            signal(g_target_in, device)
+
     pl.when((x_path > 0) & late)(lambda: signal(x_relay_in, x_source))
     pl.when((g_path > 0) & late)(lambda: signal(g_relay_in, g_source))
     for d in range(TENSOR - 1):
@@ -208,7 +213,7 @@
     wanted = order[lax.rem(s + 1, SECTIONS)]
     xs[...] = pair[wanted]
 
-    pl.when(place == 15)(lambda: start(x_split[:4]))
+    pl.when(place == 15)(lambda: start(x_split + g_copies))
 
     @pl.when(x != 7)
     def _():
@@ -252,7 +257,7 @@
     xstat[...] = totals[1:2]
 
     pl.when(x != 7)(lambda: start([x_total] + x_copies[4:]))
-    pl.when(place == 15)(lambda: start([x_total] + x_split[4:] + g_copies))
+    pl.when(place == 15)(lambda: start([x_total]))
 
     scale_row = lax.rsqrt(totals[0:1] / D + EPSILON)
     scale = as_columns(scale_row)
@@ -295,12 +300,13 @@
         dkv[koff : koff + HEAD, HEAD : 2 * HEAD] += dot(pbt[:, at], grads, (1, 0))
 
     dkv[...] = jnp.zeros_like(dkv)
+    pl.when(g_path > 0)(lambda: pl.semaphore_wait(g_target_in, 1))
     serve(0)
     for copy in g_copies[:4]:
         copy.wait_recv()
     backward(GROUPS[0][1])
     key_grads(GROUPS[0])
-    pl.when(x == 7)(lambda: serve(1))
+    serve(1)
     for copy in g_copies[4:]:
         copy.wait_recv()
     for group in GROUPS[1:]:
@@ -318,7 +324,6 @@
     cstat[t, 0:1, :] = as_row(total)
     c_sends = to_peers(cstat, csend, crecv)
     start(c_sends)
-    pl.when(x != 7)(lambda: serve(1))
 
     def finish_backward():
         from_peers(cstat, csend, crecv)
@@ -396,7 +401,7 @@
             pltpu.VMEM((1, SEQ), F32), pltpu.VMEM((1, SEQ), F32),
             dma((7,)), dma((parts,)), dma((parts,)), dma((parts,)), dma((parts,)),
             dma((TENSOR - 1,)), dma((TENSOR,)), dma((TENSOR - 1,)), dma((TENSOR,)), dma, dma,
-            regular, regular, regular, regular, regular,
+            regular, regular, regular, regular, regular, regular,
             held, held, dma((2,)), dma((2,)), dma((2,)), dma((2,)),
         ],
         compiler_params=pltpu.CompilerParams(collective_id=0, has_side_effects=True, vmem_limit_bytes=24 << 20),

time: 46.6 us -> 42.1 us (0.903)
  Pallas kernels: 45.8 us -> 40.9 us
    pallas_call x1, Pallas kernels: 44.9 us -> 40 us  [on_device(): pl.pallas_call(kernel, out_shape=(rows, rows), in_specs=[hbm] * 8, out_sp...]
where the time goes in v4:
time: 42.1 us; the launch traced here: 41.5 us
  Pallas kernels  40.9 us (97%)
  between operations  0.64 us (2%)
    pallas_call x1, Pallas kernels, on_device(): pl.pallas_call(kernel, out_shape=(rows, rows), in_specs=[hbm] * 8, out_sp...  40 us
    pallas_call x1, Pallas kernels, on_device(): pl.pallas_call(write_out, out_shape=(rows, rows), in_specs=[vmem, vmem],...  0.89 us

profile of v4, /device:TPU:1, one launch (start us, length us, event | category | flops | bytes accessed | tf_op | source)
XLA Modules:
  0.0 41.5 jit_solution(15712671026419336926)
XLA Ops:
  0.6 40.0 %shard_map.95 = (bf16[192,1024]{1,0:T(8,128)(2,1)S(1)}, bf16[192,1024]{1,0:T(8,128)(2,1)S(1)}) custom-call(s32[128]{0:T(128)} %order_hbm.1, s32[2,192]{1,0:T(2,128)} %segments_hbm.1, bf16[2,192,1024]{2,1,0:T(8,128)(2,1)} %bitcast.7, bf16[192,1024]{1,0:T(8,128)(2,1)} %bitcast.8, bf16[192,1024]{1,0:T(8,128)(2,1)} %bitcast.9, f32[1,1024]{1,0:T(1,128)} %gain_hbm.1, ...), custom_call_target="tpu_custom_call" | custom-call | tf_op jit(solution)/shard_map/pallas_call | solution.py:386
  40.7 0.9 %shard_map.96 = (bf16[192,1024]{1,0:T(8,128)(2,1)}, bf16[192,1024]{1,0:T(8,128)(2,1)}) custom-call(bf16[192,1024]{1,0:T(8,128)(2,1)S(1)} %get-tuple-element.6.first, bf16[192,1024]{1,0:T(8,128)(2,1)S(1)} %get-tuple-element.7.second), custom_call_target="tpu_custom_call" | custom-call | tf_op jit(solution)/shard_map/pallas_call | solution.py:409

commit v5 on v4

--- a/solution.py
+++ b/solution.py
@@ -197,16 +197,20 @@
     pl.when((x != 0) & (place != 15))(lambda: start(g_copies))
     pl.when(place == 8)(lambda: start(g_split))
 
-    def serve(j):
-        def one(path, held, held_recv, held_send, dst, recv, target):
-            @pl.when(path > 0)
-            def _():
-                at, n = HELD[j]
-                remote(held.at[pl.ds(at, n)], held.at[pl.ds(at, n)], held_send.at[j], held_recv.at[j], target).wait_recv()
-                from_relay(j, path, held, dst, held_send, recv, target).start()
-
-        one(g_path, g_held, g_held_recv, g_held_send, gin, grecv, g_target)
-        one(x_path, x_held, x_held_recv, x_held_send, xin, xrecv, x_target)
+    def serve(j, path, held, held_recv, held_send, dst, recv, target):
+        at, n = HELD[j]
+        remote(held.at[pl.ds(at, n)], held.at[pl.ds(at, n)], held_send.at[j], held_recv.at[j], target).wait_recv()
+        from_relay(j, path, held, dst, held_send, recv, target).start()
+
+    def serve_g():
+        pl.semaphore_wait(g_target_in, 1)
+        for j in range(2):
+            serve(j, g_path, g_held, g_held_recv, g_held_send, gin, grecv, g_target)
+
+    def serve_x(j):
+        serve(j, x_path, x_held, x_held_recv, x_held_send, xin, xrecv, x_target)
+
+    own_first = (place == 0) & (s != 0)
 
     loads[0].wait()
     loads[1].wait()
@@ -300,13 +304,14 @@
         dkv[koff : koff + HEAD, HEAD : 2 * HEAD] += dot(pbt[:, at], grads, (1, 0))
 
     dkv[...] = jnp.zeros_like(dkv)
-    pl.when(g_path > 0)(lambda: pl.semaphore_wait(g_target_in, 1))
-    serve(0)
+    pl.when((g_path > 0) & jnp.logical_not(own_first))(serve_g)
+    pl.when(x == 7)(lambda: serve_x(0))
     for copy in g_copies[:4]:
         copy.wait_recv()
     backward(GROUPS[0][1])
     key_grads(GROUPS[0])
-    serve(1)
+    pl.when((x_path > 0) & (x != 7))(lambda: serve_x(0))
+    pl.when(x_path > 0)(lambda: serve_x(1))
     for copy in g_copies[4:]:
         copy.wait_recv()
     for group in GROUPS[1:]:
@@ -324,6 +329,7 @@
     cstat[t, 0:1, :] = as_row(total)
     c_sends = to_peers(cstat, csend, crecv)
     start(c_sends)
+    pl.when(own_first)(serve_g)
 
     def finish_backward():
         from_peers(cstat, csend, crecv)
@@ -333,7 +339,8 @@
             at = slice(h * HEAD, (h + 1) * HEAD)
             bwd_out[:, at] = (dn[:, at] - y[:, at].astype(F32) * pull).astype(BF16)
 
-    pl.when(x == 0)(finish_backward)
+    finish_first = (x == 0) & (s != 0)
+    pl.when(finish_first)(finish_backward)
 
     for copy in x_copies[:4]:
         copy.wait_recv()
@@ -352,7 +359,7 @@
                 mixed = dot(p, kvx[koff : koff + HEAD, HEAD : 2 * HEAD], (0, 0)).astype(BF16).astype(F32)
                 put(fwd_out, unit, (take(xin, unit).astype(F32) + mixed).astype(BF16))
 
-    pl.when(x != 0)(finish_backward)
+    pl.when(jnp.logical_not(finish_first))(finish_backward)
 
     for copy in stat_sends + g_copies + x_copies + [x_total] + c_sends:
         copy.wait_send()

time: 42.1 us -> 41.9 us (level)
  no operation moved by 1% of the time
where the time goes in v5:
time: 41.9 us; the launch traced here: 41.7 us
  Pallas kernels  41.1 us (98%)
  between operations  0.64 us (2%)
    pallas_call x1, Pallas kernels, on_device(): pl.pallas_call(kernel, out_shape=(rows, rows), in_specs=[hbm] * 8, out_sp...  40.2 us
    pallas_call x1, Pallas kernels, on_device(): pl.pallas_call(write_out, out_shape=(rows, rows), in_specs=[vmem, vmem],...  0.89 us

profile of v5, /device:TPU:1, one launch (start us, length us, event | category | flops | bytes accessed | tf_op | source)
XLA Modules:
  0.0 41.7 jit_solution(17358791908149889189)
XLA Ops:
  0.6 40.2 %shard_map.95 = (bf16[192,1024]{1,0:T(8,128)(2,1)S(1)}, bf16[192,1024]{1,0:T(8,128)(2,1)S(1)}) custom-call(s32[128]{0:T(128)} %order_hbm.1, s32[2,192]{1,0:T(2,128)} %segments_hbm.1, bf16[2,192,1024]{2,1,0:T(8,128)(2,1)} %bitcast.7, bf16[192,1024]{1,0:T(8,128)(2,1)} %bitcast.8, bf16[192,1024]{1,0:T(8,128)(2,1)} %bitcast.9, f32[1,1024]{1,0:T(1,128)} %gain_hbm.1, ...), custom_call_target="tpu_custom_call" | custom-call | tf_op jit(solution)/shard_map/pallas_call | solution.py:393
  40.8 0.9 %shard_map.96 = (bf16[192,1024]{1,0:T(8,128)(2,1)}, bf16[192,1024]{1,0:T(8,128)(2,1)}) custom-call(bf16[192,1024]{1,0:T(8,128)(2,1)S(1)} %get-tuple-element.6.first, bf16[192,1024]{1,0:T(8,128)(2,1)S(1)} %get-tuple-element.7.second), custom_call_target="tpu_custom_call" | custom-call | tf_op jit(solution)/shard_map/pallas_call | solution.py:416

commit v6 on v5

--- a/solution.py
+++ b/solution.py
@@ -13,9 +13,12 @@
 MESH = pl.DeviceIdType.MESH
 F32, BF16 = jnp.float32, jnp.bfloat16
 CHUNKS = ((0, 128), (128, 64))
-PIECES = tuple((i * 32, 32) for i in range(4)) + tuple((128 + i * 16, 16) for i in range(4))
-HELD = ((0, 32), (32, 16))
-X_RELAYS, G_RELAYS = (7, 6, 1), (0, 1, 6)
+PATHS, FIRST = 6, 8
+PIECES = tuple((i * 16, 16) for i in range(2 * PATHS))
+PATH_OF = tuple(range(PATHS)) + tuple((i + PATHS - 2) % PATHS for i in range(PATHS))
+HELD = ((0, 16), (16, 16))
+X_RELAYS, G_RELAYS = (7, 6, 1, 5, 2), (0, 1, 6, 2, 5)
+NEAR = 3
 
 UNITS = tuple((0, 128, (h,), 0) for h in range(HEADS)) + tuple(
     (q, 32, tuple(range(h, h + 4)), q - 96) for q in (128, 160) for h in (0, 4)
@@ -111,8 +114,8 @@
     def relays(b, columns):
         return [(partner(b) * 8 + column, t) for column in columns]
 
-    x_path = jnp.where(x == 7, 1, jnp.where(x == 6, 2, jnp.where(x == 1, 3, 0)))
-    g_path = jnp.where(x == 0, 1, jnp.where(x == 1, 2, jnp.where(x == 6, 3, 0)))
+    x_path = sum(jnp.where(x == column, path + 1, 0) for path, column in enumerate(X_RELAYS))
+    g_path = sum(jnp.where(x == column, path + 1, 0) for path, column in enumerate(G_RELAYS))
     x_source, x_target = (partner(block) * 8 + 7, t), (lax.rem(partner(block) * 8 + 8, SECTIONS), t)
     g_source, g_target = (partner(block) * 8, t), (lax.rem(partner(block) * 8 + SECTIONS - 1, SECTIONS), t)
 
@@ -134,7 +137,8 @@
     pl.when(place == 7)(lambda: greet(relays(block, X_RELAYS)))
     pl.when(place == 0)(lambda: greet(relays(block, G_RELAYS)))
     pl.when(x == 0)(lambda: greet(relays(lax.rem(s + SECTIONS - 1, SECTIONS) // 8, X_RELAYS)))
-    pl.when(g_path > 0)(lambda: greet([g_target]))
+    pl.when((g_path > 0) & (g_path <= NEAR))(lambda: greet([g_target]))
+    pl.when(x == 7)(lambda: greet(relays(lax.rem(s + 1, SECTIONS) // 8, G_RELAYS[NEAR:])))
     loads = [
         pltpu.make_async_copy(produced, pair, load_sem.at[0]),
         pltpu.make_async_copy(order_hbm, order, load_sem.at[1]),
@@ -148,8 +152,8 @@
         load.start()
     x_role, g_role = jnp.where(x_path > 0, 1, 0), jnp.where(g_path > 0, 1, 0)
     greeted = (
-        t + jnp.where(place != 0, 1, 0) + jnp.where(place == 15, 4, 0) + jnp.where(place == 8, 3, 0)
-        + jnp.where(x == 7, 3, 0) + x_role + jnp.where(late, x_role + g_role, 0)
+        t + jnp.where(place != 0, 1, 0) + jnp.where(place == 15, 1 + len(X_RELAYS), 0) + jnp.where(place == 8, len(G_RELAYS), 0)
+        + jnp.where(x == 7, NEAR, 0) + jnp.where(g_path > NEAR, 1, 0) + x_role + jnp.where(late, x_role + g_role, 0)
     )
     pl.when(greeted > 0)(lambda: pl.semaphore_wait(barrier, greeted))
     pl.when(place != 0)(lambda: signal(next_in, prv))
@@ -157,7 +161,7 @@
 
     @pl.when(x == 7)
     def _():
-        for device in relays(lax.rem(s + 1, SECTIONS) // 8, G_RELAYS):
+        for device in relays(lax.rem(s + 1, SECTIONS) // 8, G_RELAYS[:NEAR]):
             signal(g_target_in, device)
 
     pl.when((x_path > 0) & late)(lambda: signal(x_relay_in, x_source))
@@ -175,19 +179,24 @@
         return remote(src.at[pl.ds(q, n)], dst.at[pl.ds(q, n)], send.at[i], recv.at[i], device)
 
     def to_relay(i, src, held, send, recv, device):
-        (q, n), (at, _) = PIECES[i], HELD[i // 4]
-        return remote(src.at[pl.ds(q, n)], held.at[pl.ds(at, n)], send.at[i], recv.at[i // 4], device)
+        (q, n), (at, _) = PIECES[i], HELD[i // PATHS]
+        return remote(src.at[pl.ds(q, n)], held.at[pl.ds(at, n)], send.at[i], recv.at[i // PATHS], device)
 
     def from_relay(j, path, held, dst, send, recv, device):
         at, n = HELD[j]
-        rows = pl.ds(pl.multiple_of(128 * j + path * n, 16), n)
-        return remote(held.at[pl.ds(at, n)], dst.at[rows], send.at[j], recv.at[4 * j + path], device)
-
-    g_copies = [straight(i, gs, gin, gsend, grecv, prv) for i in range(8)]
-    x_copies = [straight(i, xs, xin, xsend, xrecv, nxt) for i in range(8)]
+        piece = PATHS + lax.rem(path + 2, PATHS) if j else path
+        rows = pl.ds(pl.multiple_of(piece * n, 16), n)
+        return remote(held.at[pl.ds(at, n)], dst.at[rows], send.at[j], recv.at[piece], device)
+
+    g_copies = [straight(i, gs, gin, gsend, grecv, prv) for i in range(len(PIECES))]
+    x_copies = [straight(i, xs, xin, xsend, xrecv, nxt) for i in range(len(PIECES))]
     g_devices, x_devices = relays(block, G_RELAYS), relays(block, X_RELAYS)
-    g_split = [g_copies[i] if i % 4 == 0 else to_relay(i, gs, g_held, gsend, g_held_recv, g_devices[i % 4 - 1]) for i in range(8)]
-    x_split = [x_copies[i] if i % 4 == 0 else to_relay(i, xs, x_held, xsend, x_held_recv, x_devices[i % 4 - 1]) for i in range(8)]
+    g_split = [
+        to_relay(i, gs, g_held, gsend, g_held_recv, g_devices[p - 1]) if p else g_copies[i] for i, p in enumerate(PATH_OF)
+    ]
+    x_split = [
+        to_relay(i, xs, x_held, xsend, x_held_recv, x_devices[p - 1]) if p else x_copies[i] for i, p in enumerate(PATH_OF)
+    ]
     x_total = remote(xstat, xstat_in, tsend, trecv, nxt)
 
     def start(copies):
@@ -203,7 +212,7 @@
         from_relay(j, path, held, dst, held_send, recv, target).start()
 
     def serve_g():
-        pl.semaphore_wait(g_target_in, 1)
+        pl.when(g_path <= NEAR)(lambda: pl.semaphore_wait(g_target_in, 1))
         for j in range(2):
             serve(j, g_path, g_held, g_held_recv, g_held_send, gin, grecv, g_target)
 
@@ -222,7 +231,7 @@
     @pl.when(x != 7)
     def _():
         pl.semaphore_wait(next_in, 1)
-        start(x_copies[:4])
+        start(x_copies[:FIRST])
 
     loads[2].wait()
 
@@ -260,7 +269,7 @@
     totals = jnp.sum(stat[...], axis=0)
     xstat[...] = totals[1:2]
 
-    pl.when(x != 7)(lambda: start([x_total] + x_copies[4:]))
+    pl.when(x != 7)(lambda: start([x_total] + x_copies[FIRST:]))
     pl.when(place == 15)(lambda: start([x_total]))
 
     scale_row = lax.rsqrt(totals[0:1] / D + EPSILON)
@@ -275,13 +284,13 @@
     @pl.when(place == 0)
     def _():
         pl.semaphore_wait(previous_in, 1)
-        pl.semaphore_wait(g_relay_in, 3)
+        pl.semaphore_wait(g_relay_in, len(G_RELAYS))
         start(g_split)
 
     @pl.when(place == 7)
     def _():
         pl.semaphore_wait(next_in, 1)
-        pl.semaphore_wait(x_relay_in, 3)
+        pl.semaphore_wait(x_relay_in, len(X_RELAYS))
         start([x_total] + x_split)
 
     def backward(units):
@@ -306,13 +315,13 @@
     dkv[...] = jnp.zeros_like(dkv)
     pl.when((g_path > 0) & jnp.logical_not(own_first))(serve_g)
     pl.when(x == 7)(lambda: serve_x(0))
-    for copy in g_copies[:4]:
+    for copy in g_copies[:FIRST]:
         copy.wait_recv()
     backward(GROUPS[0][1])
     key_grads(GROUPS[0])
     pl.when((x_path > 0) & (x != 7))(lambda: serve_x(0))
     pl.when(x_path > 0)(lambda: serve_x(1))
-    for copy in g_copies[4:]:
+    for copy in g_copies[FIRST:]:
         copy.wait_recv()
     for group in GROUPS[1:]:
         backward(group[1])
@@ -342,13 +351,13 @@
     finish_first = (x == 0) & (s != 0)
     pl.when(finish_first)(finish_backward)
 
-    for copy in x_copies[:4]:
+    for copy in x_copies[:FIRST]:
         copy.wait_recv()
     x_total.wait_recv()
     scale_f = as_columns(lax.rsqrt(xstat_in[...] / D + EPSILON))
     for i, (q, n) in enumerate(CHUNKS):
         if i:
-            for copy in x_copies[4:]:
+            for copy in x_copies[FIRST:]:
                 copy.wait_recv()
         normalized(xin, nx, (q, n), scale_f, gain)
         kvx[q : q + n] = dot(nx[q : q + n], w[...], (1, 0)).astype(BF16)
@@ -389,7 +398,7 @@
     wide = len(UNITS) * HEAD
     dma, regular = pltpu.SemaphoreType.DMA, pltpu.SemaphoreType.REGULAR
     parts = len(PIECES)
-    held = pltpu.VMEM((48, WIDTH), BF16)
+    held = pltpu.VMEM((32, WIDTH), BF16)
     forward_out, input_grad = pl.pallas_call(
         kernel,
         out_shape=(rows, rows),

time: 41.9 us -> 41.9 us (level)
  the two profiles are of different devices: /device:TPU:1 before, /device:TPU:15 now
where the time goes in v6:
time: 41.9 us; the launch traced here: 41.7 us
  Pallas kernels  41.1 us (98%)
  between operations  0.64 us (2%)
    pallas_call x1, Pallas kernels, on_device(): pl.pallas_call(kernel, out_shape=(rows, rows), in_specs=[hbm] * 8, out_sp...  40.2 us
    pallas_call x1, Pallas kernels, on_device(): pl.pallas_call(write_out, out_shape=(rows, rows), in_specs=[vmem, vmem],...  0.89 us

profile of v6, /device:TPU:15, one launch (start us, length us, event | category | flops | bytes accessed | tf_op | source)
XLA Modules:
  0.0 41.7 jit_solution(8566313531609102408)
XLA Ops:
  0.6 40.2 %shard_map.95 = (bf16[192,1024]{1,0:T(8,128)(2,1)S(1)}, bf16[192,1024]{1,0:T(8,128)(2,1)S(1)}) custom-call(s32[128]{0:T(128)} %order_hbm.1, s32[2,192]{1,0:T(2,128)} %segments_hbm.1, bf16[2,192,1024]{2,1,0:T(8,128)(2,1)} %bitcast.7, bf16[192,1024]{1,0:T(8,128)(2,1)} %bitcast.8, bf16[192,1024]{1,0:T(8,128)(2,1)} %bitcast.9, f32[1,1024]{1,0:T(1,128)} %gain_hbm.1, ...), custom_call_target="tpu_custom_call" | custom-call | tf_op jit(solution)/shard_map/pallas_call | solution.py:402
  40.8 0.9 %shard_map.96 = (bf16[192,1024]{1,0:T(8,128)(2,1)}, bf16[192,1024]{1,0:T(8,128)(2,1)}) custom-call(bf16[192,1024]{1,0:T(8,128)(2,1)S(1)} %get-tuple-element.6.first, bf16[192,1024]{1,0:T(8,128)(2,1)S(1)} %get-tuple-element.7.second), custom_call_target="tpu_custom_call" | custom-call | tf_op jit(solution)/shard_map/pallas_call | solution.py:425
